TPU v7x, 128 devices: a whole 4x4x4 slice. The times are simulated.
128 devices in a mesh: box: 4 (over y), samp: 32 (over x, z, core).
Axes of the slice: x: 4, y: 4, z: 4, core: 2. Of those that a mesh axis runs over, the one named last changes fastest.
Arguments:
- density: bfloat16 [2048, 2, 128], P(('box', 'samp')), may hold values from -6 to 6
- radiate: bfloat16 [2048, 128, 1024], P(('box', 'samp')), may hold values from -0.5 to 0.5
- receive: bfloat16 [2048, 128, 1024], P(('box', 'samp')), may hold values from -0.1875 to 0.1875
- near_tiles: bfloat16 [28672, 2, 128, 128], P(('box', 'samp')), may hold values from -0.109375 to 0.109375
- near_src: int32 [2048, 27], P(('box', 'samp')), may hold values from 0 to 2048, as said below
- near_tile: int32 [2048, 27], P(('box', 'samp')), may hold values from 0 to 28672, as said below
- send_box: int32 [128, 128, 4], P(('box', 'samp')), may hold values from 0 to 16, as said below
- distant_pattern_slot: int32 [2048, 189], P(('box', 'samp')), may hold values from 0 to 512, as said below
- far_type: int32 [2048, 189], P(('box', 'samp')), may hold values from 0 to 315
- trans_lo: bfloat16 [316, 2, 512], replicated, may hold values from -0.4375 to 0.4375
- interp_matrix: bfloat16 [512, 2048], replicated, may hold values from -0.25 to 0.25
- shifts: float32 [8, 2, 2048], replicated, may hold values from -2 to 2
- par_far: int32 [256, 189], P('box'), may hold values from 0 to 256, as said below
- par_type: int32 [256, 189], P('box'), may hold values from 0 to 315
- trans_hi: bfloat16 [316, 2, 2048], replicated, may hold values from -0.4375 to 0.4375
Outputs:
- field: float32 [2048, 2, 128], P(('box', 'samp'))
Inputs may be any that keep to these rules, and one draw needn't show every extreme that they name: `send_box`: entries equal to 16 are empty and come last in a slot row. A sender fills slots for a receiver only if it lies within 8 device numbers of it, or is 64, 32 or 16 device numbers away cyclically; for every other pair all slots are empty. One device sends 4 patterns to another in every draw, and some device receives 4 from every device that fills slots for it. `distant_pattern_slot`: the value 128 * 4 marks an empty entry; empty entries come last in a row; every other entry names a non-empty slot that its sender fills for the box's device; at least 94 entries of a row are non-empty. `near_src`: the value 2048 marks an empty entry; empty entries come last in a row; a source box lies on the box's own device or on the device of index one lower or one higher. `near_tile`: empty where near_src is; every other entry names a tile of the box's own device, and the non-empty entries of one device's boxes name each of its 224 tiles once. `par_far`: the value 256 marks an empty entry; empty entries come last in a row; at least 94 entries of a row are non-empty.
All inputs are finite; a program needn't handle non-finite values.
Results may differ from a plain program's by a relative error of at most 0.0065.
Values may be sent and summed in bfloat16 or wider, within the bound.
A program may use at most 128 MiB of HBM per device.

v0:
```python
import jax
import jax.numpy as jnp
from jax import lax
from jax.sharding import PartitionSpec as P


def shifted(value, axis, steps):
    count = lax.axis_size(axis)
    first, last = (max(0, -steps), min(count, count - steps))
    return lax.ppermute(value, axis, [(source, source + steps) for source in range(first, last)])


def radiated(density, radiate):
    half_width = radiate.shape[-1] // 2
    matvec_result = jnp.einsum("lmq,lqj->lmj", density, radiate, preferred_element_type=jnp.float32)
    real_part = matvec_result[:, 0, :half_width] - matvec_result[:, 1, half_width:]
    imag_part = matvec_result[:, 0, half_width:] + matvec_result[:, 1, :half_width]
    return jnp.stack([real_part, imag_part], 1)


def pick_rows(table, index):
    selector = (index[..., None] == jnp.arange(table.shape[0], dtype=jnp.int32)).astype(table.dtype)
    return jnp.einsum("...r,rw->...w", selector, table, preferred_element_type=jnp.float32)


def translated_flat(pattern_rows, operator_rows, width):
    real_part = jnp.sum(
        operator_rows[..., :width] * pattern_rows[..., :width]
        - operator_rows[..., width:] * pattern_rows[..., width:],
        -2,
    )
    imag_part = jnp.sum(
        operator_rows[..., :width] * pattern_rows[..., width:]
        + operator_rows[..., width:] * pattern_rows[..., :width],
        -2,
    )
    return jnp.stack([real_part, imag_part], -2)


def shifted_sum(interpolated, shifts):
    width = interpolated.shape[-1]
    grouped = interpolated.reshape(-1, 8, 2, width)
    real_part = jnp.sum(grouped[:, :, 0] * shifts[:, 0] - grouped[:, :, 1] * shifts[:, 1], 1)
    imag_part = jnp.sum(grouped[:, :, 0] * shifts[:, 1] + grouped[:, :, 1] * shifts[:, 0], 1)
    return jnp.stack([real_part, imag_part], 1)


def spread_down(incoming_hi, shifts):
    parent = incoming_hi[:, None]
    real_part = shifts[None, :, 0] * parent[:, :, 0] + shifts[None, :, 1] * parent[:, :, 1]
    imag_part = shifts[None, :, 0] * parent[:, :, 1] - shifts[None, :, 1] * parent[:, :, 0]
    stacked = jnp.stack([real_part, imag_part], 2)
    return stacked.reshape(-1, 2, incoming_hi.shape[-1]).astype(jnp.bfloat16)


def received_field(receive, incoming):
    real_in = incoming[:, 0]
    imag_in = incoming[:, 1]
    blending_operator = jnp.stack(
        [jnp.concatenate([real_in, -imag_in], -1), jnp.concatenate([imag_in, real_in], -1)], 1
    )
    return jnp.einsum(
        "mws,mis->miw", receive, blending_operator, preferred_element_type=jnp.float32
    )


def on_device(
    density,
    radiate,
    receive,
    near_tiles,
    near_src,
    near_tile,
    send_box,
    distant_pattern_slot,
    far_type,
    trans_lo,
    interp_matrix,
    shifts,
    par_far,
    par_type,
    trans_hi,
):
    box_count = density.shape[0]
    panel_count = density.shape[2]
    box_groups = lax.axis_size("box")
    samp_count = lax.axis_size("samp")
    devices = box_groups * samp_count
    position = lax.axis_index("box") * samp_count + lax.axis_index("samp")
    slot_count = send_box.shape[2]
    type_count = trans_lo.shape[0]
    pattern_lo = radiated(density, radiate).astype(jnp.bfloat16)
    width_lo = pattern_lo.shape[-1]
    flat_lo = jnp.concatenate(
        [pattern_lo.reshape(box_count, 2 * width_lo), jnp.zeros((1, 2 * width_lo), jnp.bfloat16)], 0
    )
    outgoing = pick_rows(flat_lo, send_box[0]).astype(jnp.bfloat16)
    arrived = lax.all_to_all(outgoing, ("box", "samp"), split_axis=0, concat_axis=0, tiled=True)
    lower_density = shifted(density, ("box", "samp"), 1)
    upper_density = shifted(density, ("box", "samp"), -1)
    level_window = jnp.concatenate(
        [lower_density, density, upper_density, jnp.zeros((1, 2, panel_count), jnp.bfloat16)], 0
    )
    overall_box_count = box_count * devices
    near_live = near_src < overall_box_count
    local_source = jnp.where(near_live, near_src - (position - 1) * box_count, 3 * box_count)
    tile_total = near_tiles.shape[0]
    local_tile = jnp.where(near_live, near_tile - position * tile_total, tile_total)
    owners = jnp.broadcast_to(jnp.arange(box_count, dtype=jnp.int32)[:, None], near_src.shape)
    tile_owner = (
        jnp.full((tile_total,), box_count, jnp.int32)
        .at[local_tile.reshape(-1)]
        .set(owners.reshape(-1), mode="drop")
    )
    tile_source = (
        jnp.full((tile_total,), 3 * box_count, jnp.int32)
        .at[local_tile.reshape(-1)]
        .set(local_source.reshape(-1), mode="drop")
    )
    source_values = level_window[tile_source]
    matvec_result = jnp.einsum(
        "taij,tbj->tabi", near_tiles, source_values, preferred_element_type=jnp.float32
    )
    contrib = jnp.stack(
        [
            matvec_result[:, 0, 0] - matvec_result[:, 1, 1],
            matvec_result[:, 0, 1] + matvec_result[:, 1, 0],
        ],
        1,
    )
    onehot = (tile_owner[:, None] == jnp.arange(box_count, dtype=jnp.int32)[None, :]).astype(
        jnp.float32
    )
    close_range_field = jnp.einsum("tb,tcp->bcp", onehot, contrib, precision=lax.Precision.HIGHEST)
    received = jnp.concatenate(
        [
            arrived.reshape(devices * slot_count, 2 * width_lo),
            jnp.zeros((1, 2 * width_lo), jnp.bfloat16),
        ],
        0,
    )
    far_rows = pick_rows(received, distant_pattern_slot)
    operator_rows = pick_rows(trans_lo.reshape(type_count, 2 * width_lo), far_type)
    incoming_lo = translated_flat(far_rows, operator_rows, width_lo)
    interpolated = jnp.einsum(
        "gcq,qh->gch", pattern_lo, interp_matrix, preferred_element_type=jnp.float32
    )
    parents_own = shifted_sum(interpolated, shifts).astype(jnp.bfloat16)
    per_device = parents_own.shape[0]
    everyone = lax.all_gather(parents_own, ("box", "samp"), axis=0, tiled=True)
    width_hi = everyone.shape[-1]
    start_row = lax.axis_index("samp") * per_device
    own_far = lax.dynamic_slice_in_dim(par_far, start_row, per_device, 0)
    own_type = lax.dynamic_slice_in_dim(par_type, start_row, per_device, 0)
    padded_hi = jnp.concatenate([everyone, jnp.zeros((1, 2, width_hi), jnp.bfloat16)], 0)
    parent_rows = pick_rows(padded_hi.reshape(-1, 2 * width_hi), own_far)
    parent_ops = pick_rows(trans_hi.reshape(type_count, 2 * width_hi), own_type)
    incoming_hi = translated_flat(parent_rows, parent_ops, width_hi)
    down = spread_down(incoming_hi, shifts)
    from_parent = jnp.einsum("gch,qh->gcq", down, interp_matrix, preferred_element_type=jnp.float32)
    incoming = (incoming_lo + from_parent).astype(jnp.bfloat16)
    far_field = received_field(receive, incoming)
    return 0.5 * density.astype(jnp.float32) + close_range_field + far_field


def solution(mesh):
    return jax.shard_map(
        on_device,
        mesh=mesh,
        in_specs=(
            P(("box", "samp"), None, None),
            P(("box", "samp"), None, None),
            P(("box", "samp"), None, None),
            P(("box", "samp"), None, None, None),
            P(("box", "samp"), None),
            P(("box", "samp"), None),
            P(("box", "samp"), None, None),
            P(("box", "samp"), None),
            P(("box", "samp"), None),
            P(),
            P(),
            P(),
            P("box", None),
            P("box", None),
            P(),
        ),
        out_specs=P(("box", "samp"), None, None),
        check_vma=False,
    )
```

profile of v0, /device:TPU:1, one launch (start us, length us, event | category | flops | bytes accessed | tf_op | source)
XLA Modules:
  0.0 121.8 jit_solution(11651738189777783431)
XLA Ops:
  6.5 5.1 %collective-permute-start = (bf16[16,2,128]{2,1,0:T(2,128)(2,1)}, bf16[16,2,128]{2,1,0:T(2,128)(2,1)S(1)}, u32[]{:S(2)}, u32[]{:S(2)}) collective-permute-start(bf16[16,2,128]{2,1,0:T(2,128)(2,1)} %param.15), channel_id=1, source_target_pairs={{0,1},{1,2},{2,3},{3,4},{4,5},{5,6},{6,7},{7,8},{8,9},{9,10},{10,1... | collective-permute-start | bytes 24584 | tf_op jit(solution)/shard_map/ppermute | solution.py:10
  11.6 1.9 %collective-permute-start.1 = (bf16[16,2,128]{2,1,0:T(2,128)(2,1)}, bf16[16,2,128]{2,1,0:T(2,128)(2,1)S(1)}, u32[]{:S(2)}, u32[]{:S(2)}) collective-permute-start(bf16[16,2,128]{2,1,0:T(2,128)(2,1)} %param.15), channel_id=1, source_target_pairs={{1,0},{2,1},{3,2},{4,3},{5,4},{6,5},{7,6},{8,7},{9,8},{10,9},{11,1... | collective-permute-start | bytes 24584 | tf_op jit(solution)/shard_map/ppermute | solution.py:10
  13.5 1.1 fusion.48
  14.6 2.9 %fusion.49 = f32[16,2,1024]{2,1,0:T(2,128)S(1)} fusion(bf16[16,2,128]{2,1,0:T(2,128)(2,1)} %param.15, bf16[16,128,1024]{2,1,0:T(8,128)(2,1)} %param.16), kind=kOutput, calls=%fused_computation.94 | convolution fusion | flops 8388608 | bytes 4333568 | tf_op jit(solution)/shard_map/lmq,lqj->lmj/dot_general | solution.py:15
  19.5 1.8 %copy.37 = bf16[128,4,1024]{2,1,0:T(4,128)(2,1)} copy(bf16[128,4,1024]{2,0,1:T(8,128)(2,1)S(1)} %convolution_convert_fusion) | data formatting | bytes 2097152 | tf_op jit(solution)/shard_map/convert_element_type | solution.py:97
  21.3 10.2 %all-to-all-start = ((bf16[128,4,1024]{2,1,0:T(4,128)(2,1)}), bf16[128,4,1024]{2,1,0:T(4,128)(2,1)S(1)}, u32[]{:S(2)}, u32[]{:S(2)}) async-start(bf16[128,4,1024]{2,1,0:T(4,128)(2,1)} %copy.37), calls=%async_computation | async-start | bytes 2097152 | tf_op jit(solution)/shard_map/all_to_all | solution.py:98
  31.5 7.2 %reshape.241 = bf16[316,4096,1]{1,0,2:T(8,128)(2,1)} reshape(bf16[316,2,2048]{2,1,0:T(2,128)(2,1)} %param.29) | data formatting | bytes 5177344 | tf_op jit(solution)/shard_map/reshape | solution.py:157
  38.7 2.9 %reshape.238 = bf16[316,1024,1]{1,0,2:T(8,128)(2,1)} reshape(bf16[316,2,512]{2,1,0:T(2,128)(2,1)} %param.24) | data formatting | bytes 1294336 | tf_op jit(solution)/shard_map/reshape | solution.py:143
  41.8 3.1 %scatter_custom_fusion.1 = s32[224]{0:T(256)S(1)} fusion(s32[432]{0:T(512)S(1)} %bitcast.102, s32[432]{0:T(512)S(1)} %reshape.231, s32[]{:T(128)} %constant.7.clone.1), kind=kCustom, calls=%fused_computation.81 | custom fusion | bytes 900 | tf_op jit(solution)/shard_map/scatter | solution.py:118
  44.9 0.7 constant_dynamic-slice_fusion
  45.7 6.2 %fusion.16 = f32[2,189,4096]{2,1,0:T(8,128)} fusion(bf16[316,4096,1]{1,0,2:T(8,128)(2,1)} %reshape.241, s32[2,189]{1,0:T(2,128)S(1)} %get-tuple-element.31), kind=kOutput, calls=%fused_computation.26 | convolution fusion | flops 978637440 | bytes 8783336 | tf_op jit(solution)/shard_map/...r,rw->...w/dot_general | solution.py:23
  51.9 6.4 %fusion.1 = f32[16,189,1024]{2,1,0:T(8,128)} fusion(bf16[316,1024,1]{1,0,2:T(8,128)(2,1)S(1)} %copy-done.2, s32[16,189]{1,0:T(8,128)S(1)} %copy-done.4), kind=kOutput, calls=%fused_computation.8 | convolution fusion | flops 1957991680 | bytes 13045568 | tf_op jit(solution)/shard_map/...r,rw->...w/dot_general | solution.py:23
  58.4 2.9 %scatter_custom_fusion = s32[224]{0:T(256)S(1)} fusion(s32[432]{0:T(512)S(1)} %bitcast.103, s32[432]{0:T(512)S(1)} %reshape.223, s32[]{:T(128)} %constant.17.clone.1), kind=kCustom, calls=%fused_computation.85 | custom fusion | bytes 900 | tf_op jit(solution)/shard_map/scatter | solution.py:113
  61.5 0.9 gather_fusion
  62.4 9.1 %convolution_bitcast_fusion.1 = f32[224,2,2,128]{3,2,1,0:T(2,128)S(1)} fusion(bf16[224,2,128,128]{3,2,1,0:T(8,128)(2,1)} %param.18, bf16[224,2,128]{2,1,0:T(2,128)(2,1)S(1)} %gather_fusion), kind=kOutput, calls=%fused_computation.18 | convolution fusion | flops 29360128 | bytes 15253504 | tf_op jit(solution)/shard_map/taij,tbj->tabi/dot_general | solution.py:121
  71.9 1.3 %reshape.207 = bf16[512,1024]{1,0:T(8,128)(2,1)} reshape(bf16[128,4,1024]{2,1,0:T(4,128)(2,1)S(1)} %all-to-all-done) | data formatting | bytes 2097152 | tf_op jit(solution)/shard_map/reshape | solution.py:137
  73.2 6.3 %fusion = f32[16,189,1024]{2,1,0:T(8,128)S(1)} fusion(s32[16,189]{1,0:T(8,128)S(1)} %copy-done.8, bf16[512,1024]{1,0:T(8,128)(2,1)} %reshape.207), kind=kOutput, calls=%fused_computation.4 | convolution fusion | flops 3178638336 | bytes 13446976 | tf_op jit(solution)/shard_map/...r,rw->...w/dot_general | solution.py:23
  79.5 6.5 %subtract_reduce_fusion = (f32[16,512]{1,0:T(8,128)S(1)}, f32[16,512]{1,0:T(8,128)S(1)}) fusion(f32[16,189,1024]{2,1,0:T(8,128)S(1)} %fusion, f32[16,189,1024]{2,1,0:T(8,128)} %fusion.1), kind=kLoop, calls=%fused_computation.6 | loop fusion | flops 12369920 | bytes 24838144 | tf_op jit(solution)/shard_map/reduce_sum | solution.py:27
  86.0 7.3 %all-gather.2.cloned.1.call-done = bf16[256,2,2048]{2,1,0:T(2,128)(2,1)} async-done(((bf16[2,2,2048]{2,1,0:T(2,128)(2,1)}), bf16[256,2,2048]{2,1,0:T(2,128)(2,1)}) %all-gather.2.cloned.1.call-update) | async-done | bytes 2097168 | tf_op jit(solution)/shard_map/all_gather | solution.py:150
  93.3 4.5 %concatenate.23 = bf16[257,2,2048]{2,1,0:T(2,128)(2,1)} pad(bf16[256,2,2048]{2,1,0:T(2,128)(2,1)} %all-gather.2.cloned.1.call-done, bf16[]{:T(256)} %constant.6.clone.1), padding=0_1x0_0x0_0 | pad | bytes 4202498 | tf_op jit(solution)/shard_map/concatenate | solution.py:155
  97.8 6.1 %reshape.243 = bf16[257,4096,1]{1,0,2:T(8,128)(2,1)} reshape(bf16[257,2,2048]{2,1,0:T(2,128)(2,1)} %concatenate.23) | data formatting | bytes 4210688 | tf_op jit(solution)/shard_map/reshape | solution.py:156
  103.9 3.5 %fusion.17 = f32[2,189,4096]{2,1,0:T(8,128)S(1)} fusion(bf16[257,4096,1]{1,0,2:T(8,128)(2,1)} %reshape.243, s32[2,189]{1,0:T(2,128)S(1)} %get-tuple-element.30), kind=kOutput, calls=%fused_computation.28 | convolution fusion | flops 795917184 | bytes 8300008 | tf_op jit(solution)/shard_map/...r,rw->...w/dot_general | solution.py:23
  107.4 4.6 %subtract_reduce_fusion.1 = (f32[2,2048]{1,0:T(2,128)S(1)}, f32[2,2048]{1,0:T(2,128)S(1)}) fusion(f32[2,189,4096]{2,1,0:T(8,128)S(1)} %fusion.17, f32[2,189,4096]{2,1,0:T(8,128)} %fusion.16), kind=kLoop, calls=%fused_computation.11 | loop fusion | flops 6184960 | bytes 12419072 | tf_op jit(solution)/shard_map/reduce_sum | solution.py:27
  112.9 1.2 fusion.29
  (54 shorter events, 4.4 us)
Async XLA Ops:
  6.5 11.2 %copy-start = (bf16[512,2048]{1,0:T(8,128)(2,1)S(1)}, bf16[512,2048]{1,0:T(8,128)(2,1)}, u32[]{:S(2)}) copy-start(bf16[512,2048]{1,0:T(8,128)(2,1)} %param.25) | copy-start | bytes 6291460
  6.5 12.5 %copy-start.7 = (s32[1,128,4]{1,2,0:T(4,128)S(1)}, s32[1,128,4]{1,2,0:T(4,128)}, u32[]{:S(2)}) copy-start(s32[1,128,4]{1,2,0:T(4,128)} %param.21) | copy-start | bytes 6148
  6.5 86.8 %all-gather.2.cloned.1.call-start = ((), (), s32[]{:S(2)}) async-start(), calls=%async_computation.1 | async-start | bytes 2113536 | tf_op jit(solution)/shard_map/all_gather | solution.py:150
  6.5 54.9 %collective-permute-start = (bf16[16,2,128]{2,1,0:T(2,128)(2,1)}, bf16[16,2,128]{2,1,0:T(2,128)(2,1)S(1)}, u32[]{:S(2)}, u32[]{:S(2)}) collective-permute-start(bf16[16,2,128]{2,1,0:T(2,128)(2,1)} %param.15), channel_id=1, source_target_pairs={{0,1},{1,2},{2,3},{3,4},{4,5},{5,6},{6,7},{7,8},{8,9},{9,10},{10,1... | collective-permute-start | bytes 24584 | tf_op jit(solution)/shard_map/ppermute | solution.py:10
  11.6 49.8 %collective-permute-start.1 = (bf16[16,2,128]{2,1,0:T(2,128)(2,1)}, bf16[16,2,128]{2,1,0:T(2,128)(2,1)S(1)}, u32[]{:S(2)}, u32[]{:S(2)}) collective-permute-start(bf16[16,2,128]{2,1,0:T(2,128)(2,1)} %param.15), channel_id=1, source_target_pairs={{1,0},{2,1},{3,2},{4,3},{5,4},{6,5},{7,6},{8,7},{9,8},{10,9},{11,1... | collective-permute-start | bytes 24584 | tf_op jit(solution)/shard_map/ppermute | solution.py:10
  21.3 20.3 %copy-start.5 = (s32[16,27]{1,0:T(8,128)S(1)}, s32[16,27]{1,0:T(8,128)}, u32[]{:S(2)}) copy-start(s32[16,27]{1,0:T(8,128)} %param.19) | copy-start | bytes 5188
  21.3 20.3 %copy-start.6 = (s32[16,27]{1,0:T(8,128)S(1)}, s32[16,27]{1,0:T(8,128)}, u32[]{:S(2)}) copy-start(s32[16,27]{1,0:T(8,128)} %param.20) | copy-start | bytes 5188
  21.3 50.5 %all-to-all-start = ((bf16[128,4,1024]{2,1,0:T(4,128)(2,1)}), bf16[128,4,1024]{2,1,0:T(4,128)(2,1)S(1)}, u32[]{:S(2)}, u32[]{:S(2)}) async-start(bf16[128,4,1024]{2,1,0:T(4,128)(2,1)} %copy.37), calls=%async_computation | async-start | bytes 2097152 | tf_op jit(solution)/shard_map/all_to_all | solution.py:98
  45.7 6.3 %copy-start.2 = (bf16[316,1024,1]{1,0,2:T(8,128)(2,1)S(1)}, bf16[316,1024,1]{1,0,2:T(8,128)(2,1)}, u32[]{:S(2)}) copy-start(bf16[316,1024,1]{1,0,2:T(8,128)(2,1)} %reshape.238) | copy-start | bytes 1941508
  45.7 6.3 %copy-start.4 = (s32[16,189]{1,0:T(8,128)S(1)}, s32[16,189]{1,0:T(8,128)}, u32[]{:S(2)}) copy-start(s32[16,189]{1,0:T(8,128)} %param.23) | copy-start | bytes 36292
  51.9 9.5 %copy-start.3 = (bf16[16,2,128]{2,1,0:T(2,128)(2,1)S(1)}, bf16[16,2,128]{2,1,0:T(2,128)(2,1)}, u32[]{:S(2)}) copy-start(bf16[16,2,128]{2,1,0:T(2,128)(2,1)} %param.15) | copy-start | bytes 24580
  62.4 10.8 %copy-start.8 = (s32[16,189]{1,0:T(8,128)S(1)}, s32[16,189]{1,0:T(8,128)}, u32[]{:S(2)}) copy-start(s32[16,189]{1,0:T(8,128)} %param.22) | copy-start | bytes 36292
  107.4 5.5 %copy-start.1 = (bf16[16,128,1024]{2,1,0:T(8,128)(2,1)S(1)}, bf16[16,128,1024]{2,1,0:T(8,128)(2,1)}, u32[]{:S(2)}) copy-start(bf16[16,128,1024]{2,1,0:T(8,128)(2,1)} %param.17) | copy-start | bytes 12582916
Sparse Core Ops, SparseCore 0:
  19.1 74.1 all-gather.1
where the time goes:
time: 122 us
  matrix products  37.5 us (31%)
  local copies, waits for them, and re-layouts  34.2 us (28%)
  starting transfers between devices  17.2 us (14%)
  between operations  13.7 us (11%)
  other arithmetic  12 us (10%)
  waiting for transfers between devices  7.3 us (6%)
    dot_general x5, matrix products, pick_rows(): jnp.einsum('...r,rw->...w', selector, table, preferred_element_type=jnp.f...  23 us
    reduce_sum x2, other arithmetic, translated_flat(): jnp.sum(operator_rows[..., :width] * pattern_rows[..., :width] - operator...  11.1 us
    all_to_all x1, starting transfers between devices, on_device(): lax.all_to_all(outgoing, ('box', 'samp'), split_axis=0, concat_axis=0, ti...  10.2 us
    dot_general x1, matrix products, on_device(): jnp.einsum('taij,tbj->tabi', near_tiles, source_values, preferred_element...  9.07 us
    all_gather x1, waiting for transfers between devices, on_device(): everyone = lax.all_gather(parents_own, ('box', 'samp'), axis=0, tiled=True)  7.27 us
    reshape x1, local copies, waits for them, and re-layouts, on_device(): parent_ops = pick_rows(trans_hi.reshape(type_count, 2 * width_hi), own_type)  7.17 us
    ppermute x2, starting transfers between devices, shifted(): lax.ppermute(value, axis, [(source, source + steps) for source in range(f...  6.98 us
    reshape x1, local copies, waits for them, and re-layouts, on_device(): parent_rows = pick_rows(padded_hi.reshape(-1, 2 * width_hi), own_far)  6.06 us
  transfers between devices with their start and end apart: 4, of which 1 were waited for; matrix products, arithmetic and copies ran while one was open for 51% of the time, Pallas kernels for 0%

commit v1 on v0

v1 whole, which is shorter than its diff:
```python
import functools

import jax
import jax.numpy as jnp
from jax import lax
from jax.experimental import pallas as pl
from jax.experimental.pallas import tpu as pltpu
from jax.sharding import PartitionSpec as P

F32 = jnp.float32
BF16 = jnp.bfloat16
I32 = jnp.int32
JUMPS = (16, 32, 64, 96, 112)
TPAD = 384
GROUP = 16


def nn(a, b):
    return lax.dot_general(a, b, (((1,), (0,)), ((), ())), preferred_element_type=F32)


def nt(a, b):
    return lax.dot_general(a, b, (((1,), (1,)), ((), ())), preferred_element_type=F32)


def rows_of(shape):
    return lax.broadcasted_iota(I32, shape, 0)


def lanes_of(shape):
    return lax.broadcasted_iota(I32, shape, 1)


def onehot(mask):
    return jnp.where(mask, 1.0, 0.0).astype(BF16)


def device(pos):
    return (pos // 32, pos % 32)


def kernel(
    dens, sb, near_src, near_tile, dps_in, ftype_in, pfar_in, ptype_in, shift_rows,
    radiate, receive, tiles, interp, lo_rows, hi_rows,
    out,
    dens_f, win_f, nidx, dps, ftype, pfar, ptype, shifts, lo_v, lo_f, hi_v, hi_f, tlo, thi, pat3, lo_sem, hi_sem,
    rad_v, rec_v, tile_v, int_v, window, patf, leaf_msg, leaf_in, hi_scr, one_msg, one_in, one_f,
    two_msg, two_in, hi_p, ret_msg, ret_in, down, n_lo, w_lo, p_lo, n_hi, w_hi, inc_lo, contrib, picked,
    rad_sem, rec_sem, tile_sem, int_sem, loc_sem,
    win_s, win_r, leaf_s, leaf_r, one_s, one_r, two_s, two_r, ret_s, ret_r,
):
    y = lax.axis_index("box")
    s = lax.axis_index("samp")
    me = y * 32 + s
    zc = s % 8
    yx = y * 4 + s // 8

    def rad_copy(i):
        sl = pl.ds(i * 256, 256)
        return pltpu.make_async_copy(radiate.at[sl], rad_v.at[sl], rad_sem.at[i])

    def rec_copy(i):
        sl = pl.ds(i * 256, 256)
        return pltpu.make_async_copy(receive.at[sl], rec_v.at[sl], rec_sem.at[i])

    def tile_copy(i):
        sl = pl.ds(i * GROUP, GROUP)
        return pltpu.make_async_copy(tiles.at[sl], tile_v.at[sl], tile_sem.at[i])

    int_copy = pltpu.make_async_copy(interp, int_v, int_sem)
    groups = tiles.shape[0] // GROUP

    lo_copy = pltpu.make_async_copy(lo_rows, lo_v, lo_sem)
    hi_copy = pltpu.make_async_copy(hi_rows.at[:, pl.ds((zc // 4) * 16, 16), :], hi_v, hi_sem)

    for i in range(8):
        rad_copy(i).start()
    int_copy.start()
    lo_copy.start()
    hi_copy.start()

    barrier = pltpu.get_barrier_semaphore()

    @pl.loop(1, 16)
    def _(i):
        pl.semaphore_signal(barrier, inc=1, device_id=device((me + 8 * i) % 128), device_id_type=pl.DeviceIdType.MESH)

    @pl.loop(1, 8)
    def _(i):
        pl.semaphore_signal(barrier, inc=1, device_id=device((me + i) % 128), device_id_type=pl.DeviceIdType.MESH)
        pl.semaphore_signal(barrier, inc=1, device_id=device((me + 128 - i) % 128), device_id_type=pl.DeviceIdType.MESH)

    @pl.loop(0, groups)
    def _(i):
        tile_copy(i).start()

    @pl.loop(0, 8)
    def _(i):
        rec_copy(i).start()

    def send(src, dst, ss, rs, pos):
        return pltpu.make_async_remote_copy(
            src_ref=src, dst_ref=dst, send_sem=ss, recv_sem=rs, device_id=device(pos), device_id_type=pl.DeviceIdType.MESH
        )

    dens_f[...] = dens[...].astype(F32)
    d_re = dens_f[pl.ds(0, 16, stride=2), :]
    d_im = dens_f[pl.ds(1, 16, stride=2), :]
    d_all = jnp.concatenate([d_re, d_im], 0)
    own = rows_of((32, 128)) % 16
    acc = jnp.zeros((32, 1024), F32)
    for i in range(8):
        rad_copy(i).wait()
        lhs = jnp.concatenate(
            [jnp.where(own == 2 * i + h, d_all, 0.0).astype(BF16) for h in range(2)], 1
        )
        acc = acc + nn(lhs, rad_v[i * 256 : (i + 1) * 256])
    pat = jnp.concatenate([acc[:16, :512] - acc[16:, 512:], acc[:16, 512:] + acc[16:, :512]], 0).astype(BF16)
    pat_f = pat.astype(F32)
    for m in range(2):
        for b in range(4):
            patf[pl.ds(m * 4 + b, 16, stride=8), :] = pat_f[m * 16 : (m + 1) * 16, b * 128 : (b + 1) * 128]
    pat3[...] = patf[...].reshape(16, 8, 128)
    for m in range(2):
        for b in range(16):
            shifts[m, :, b * 128 : (b + 1) * 128] = shift_rows[pl.ds(b * 2 + m, 8, stride=32), :]

    pl.semaphore_wait(barrier, 29)

    up_copy = send(dens, window.at[0], win_s.at[0], win_r.at[0], (me + 1) % 128)
    low_copy = send(dens, window.at[2], win_s.at[1], win_r.at[1], (me + 127) % 128)
    up_copy.start()
    low_copy.start()
    window[1] = dens[...]

    def fill(dst, j, receiver):
        for half in range(2):
            parts = []
            for k in range(2):
                box = jnp.minimum(sb[half * 2 + k, receiver], 15)
                parts.append(pat3[box])
            dst[j, pl.ds(half * 16, 16), :] = jnp.concatenate(parts, 0).astype(BF16)

    def near_send(j):
        return send(leaf_msg.at[j], leaf_in.at[16 - j], leaf_s.at[j], leaf_r.at[16 - j], (me + j + 120) % 128)

    def jump_send(i):
        return send(
            leaf_msg.at[17 + i], leaf_in.at[21 - i], leaf_s.at[17 + i], leaf_r.at[21 - i], (me + JUMPS[i]) % 128
        )

    int_copy.wait()
    up = nn(pat, int_v[...])
    s_re = shifts[0]
    s_im = shifts[1]
    for p in range(2):
        re = up[p * 8 : p * 8 + 8]
        im = up[16 + p * 8 : 24 + p * 8]
        vals = (
            jnp.sum(re * s_re - im * s_im, 0, keepdims=True),
            jnp.sum(re * s_im + im * s_re, 0, keepdims=True),
        )
        for m in range(2):
            for c in range(8):
                for h in range(2):
                    b = c * 2 + h
                    hi_scr[c, pl.ds(m * 4 + h * 2 + p, 1), :] = vals[m][:, b * 128 : (b + 1) * 128]
    one_msg[...] = hi_scr[...].astype(BF16)

    def one_send(i):
        peer = (zc + i) % 8
        return send(one_msg.at[peer], one_in.at[zc], one_s.at[i], one_r.at[i], yx * 8 + peer)

    @pl.loop(1, 8)
    def _(i):
        one_send(i).start()

    one_in[zc] = one_msg[zc]

    @pl.loop(0, 8)
    def _(j):
        fill(leaf_msg, j, (me + j + 120) % 128)
        near_send(j).start()

    @pl.loop(9, 17)
    def _(j):
        fill(leaf_msg, j, (me + j + 120) % 128)
        near_send(j).start()

    for i in range(5):
        fill(leaf_msg, 17 + i, (me + JUMPS[i]) % 128)
        jump_send(i).start()
    fill(leaf_in, 8, me)

    nidx[...] = jnp.full((8, 128), -1, I32)
    for g in range(16):
        at = (g % 4) * 32
        nidx[g // 4 : g // 4 + 1, at : at + 27] = near_src[g : g + 1, :]
        nidx[4 + g // 4 : 5 + g // 4, at : at + 27] = near_tile[g : g + 1, :]
    column = s // 8
    part = pl.ds(pl.multiple_of(column * 16, 16), 16)
    for held, given in ((dps, dps_in[...]), (ftype, ftype_in[...]), (pfar, pfar_in[part, :]), (ptype, ptype_in[part, :])):
        held[...] = jnp.full((16, 256), -1, I32)
        held[:, :189] = given
    lo_copy.wait()
    lo_f[:2528, :] = lo_v[...].astype(F32)
    lo_f[2528:, :] = jnp.zeros((544, 128), F32)
    for r in range(8):
        at = (r % 2) * 512 + (r // 2) * 128
        tlo[:, at : at + 128] = lo_f[pl.ds(r, TPAD, stride=8), :].astype(BF16)
    hi_copy.wait()

    @pl.loop(0, 4)
    def _(i):
        hi_f[pl.ds(pl.multiple_of(i * 1264, 16), 1264), :] = hi_v[pl.ds(i * 79, 79)].astype(F32).reshape(1264, 128)

    hi_f[5056:, :] = jnp.zeros((1088, 128), F32)
    for r in range(4):
        at = (r % 2) * 256 + (r // 2) * 128
        thi[:, at : at + 128] = hi_f[pl.ds((zc % 4) * 4 + r, TPAD, stride=16), :].astype(BF16)

    row = rows_of((96, 256))
    slot = row // 4
    delta = jnp.where(
        slot <= 16,
        slot - 8,
        jnp.where(slot == 17, 16, jnp.where(slot == 18, 32, jnp.where(slot == 19, 64, jnp.where(slot == 20, 96, 112)))),
    )
    expect = jnp.where(row < 88, ((me + delta + 128) % 128) * 4 + row % 4, -2)
    kinds = rows_of((TPAD, 256))

    @pl.loop(0, 16)
    def _(g):
        a = onehot(dps[pl.ds(g, 1), :] == expect)
        b = onehot(ftype[pl.ds(g, 1), :] == kinds)
        n_lo[pl.ds(pl.multiple_of(g * 96, 32), 96), :] = nt(a, b).astype(BF16)

    @pl.loop(1, 8)
    def _(i):
        one_send(i).wait_recv()

    one_f[...] = one_in[...].astype(F32).reshape(64, 128)
    for m in range(4):
        two_msg[m] = jnp.concatenate(
            [one_f[pl.ds(m * 2 + p, 8, stride=8), :] for p in range(2)], 0
        ).astype(BF16)

    def two_send(i):
        peer = (yx + i) % 16
        return send(two_msg, two_in.at[yx], two_s.at[i], two_r.at[i], peer * 8 + zc)

    @pl.loop(1, 16)
    def _(i):
        two_send(i).start()

    two_in[yx] = two_msg[...]

    @pl.loop(0, 4)
    def _(i):
        sl = pl.ds(pl.multiple_of(i * 384, 384), 384)
        w_lo[sl, :] = nn(n_lo[sl, :], tlo[...])

    prow = rows_of((256, 256))
    parent = (prow // 16) * 16 + (prow % 8) * 2 + (prow // 8) % 2

    @pl.loop(0, 16)
    def _(g):
        a = onehot(pfar[pl.ds(g, 1), :] == parent)
        b = onehot(ptype[pl.ds(g, 1), :] == kinds)
        n_hi[pl.ds(pl.multiple_of(g * 256, 256), 256), :] = nt(a, b).astype(BF16)

    @pl.loop(0, 8)
    def _(i):
        sl = pl.ds(pl.multiple_of(i * 512, 512), 512)
        w_hi[sl, :] = nn(n_hi[sl, :], thi[...])

    up_copy.wait_recv()
    low_copy.wait_recv()
    tile_rows = me * 224 + rows_of((224, 128))
    live = jnp.concatenate([onehot(nidx[pl.ds(4 + r, 1), :] == tile_rows) for r in range(4)], 1)
    box_rows = (me - 1) * 16 + rows_of((48, 128))
    source = jnp.concatenate([onehot(nidx[pl.ds(r, 1), :] == box_rows) for r in range(4)], 1)
    owner = jnp.concatenate(
        [onehot(rows_of((16, 128)) == 4 * r + lanes_of((16, 128)) // 32) for r in range(4)], 1
    )
    own_tile = nt(owner, live).astype(BF16)
    select = nt(live, source).astype(BF16)
    win_f[...] = window[...].astype(F32).reshape(96, 128)
    x_re = win_f[pl.ds(0, 48, stride=2), :]
    x_im = win_f[pl.ds(1, 48, stride=2), :]
    values = jnp.concatenate([x_re, -x_im, x_im, x_re], 1).astype(BF16)
    picked[...] = nn(select, values).astype(BF16)

    @pl.loop(0, groups)
    def _(grp):
        tile_copy(grp).wait()
        base = pl.multiple_of(grp * GROUP, GROUP)
        x = picked[pl.ds(base, GROUP), :]
        lhs = jnp.concatenate([x[:, :256], x[:, 256:]], 0)
        local = rows_of((2 * GROUP, 128)) % GROUP
        total = jnp.zeros((2 * GROUP, 128), F32)
        for q in range(GROUP // 2):
            pair = []
            for u in range(2):
                t = base + 2 * q + u
                pair.append(jnp.concatenate([tile_v[t, 0], tile_v[t, 1]], 1))
            res = nt(lhs, jnp.concatenate(pair, 0))
            for u in range(2):
                total = total + jnp.where(local == 2 * q + u, res[:, u * 128 : (u + 1) * 128], 0.0)
        contrib[pl.ds(base, GROUP), :] = jnp.concatenate([total[:GROUP], total[GROUP:]], 1)

    whole = contrib[...]
    high = whole.astype(BF16)
    near = nn(own_tile, high) + nn(own_tile, (whole - high.astype(F32)).astype(BF16))

    @pl.loop(1, 16)
    def _(i):
        two_send(i).wait_recv()

    for m in range(4):
        for i in range(16):
            hi_p[m, i * 16 : (i + 1) * 16, :] = two_in[i, m].astype(F32)

    @pl.loop(0, 8)
    def _(c):
        for p in range(2):
            base = pl.multiple_of((c * 2 + p) * 256, 256)
            for h in range(2):
                wr = w_hi[pl.ds(base, 256), h * 128 : (h + 1) * 128]
                wi = w_hi[pl.ds(base, 256), 256 + h * 128 : 256 + (h + 1) * 128]
                pr = hi_p[h]
                pi = hi_p[2 + h]
                ret_msg[c, pl.ds(h * 2 + p, 1), :] = jnp.sum(wr * pr - wi * pi, 0, keepdims=True)
                ret_msg[c, pl.ds(4 + h * 2 + p, 1), :] = jnp.sum(wr * pi + wi * pr, 0, keepdims=True)

    def ret_send(i):
        peer = (zc + i) % 8
        return send(ret_msg.at[peer], ret_in.at[zc], ret_s.at[i], ret_r.at[i], yx * 8 + peer)

    @pl.loop(1, 8)
    def _(i):
        ret_send(i).start()

    ret_in[zc] = ret_msg[zc]

    @pl.loop(0, 8)
    def _(j):
        near_send(j).wait_recv()

    @pl.loop(9, 17)
    def _(j):
        near_send(j).wait_recv()

    for i in range(5):
        jump_send(i).wait_recv()

    p_lo[...] = leaf_in[...].astype(F32).reshape(704, 128)

    @pl.loop(0, 16)
    def _(g):
        base = pl.multiple_of(g * 96, 32)
        reals, imags = [], []
        for b in range(4):
            wr = w_lo[pl.ds(base, 88), b * 128 : (b + 1) * 128]
            wi = w_lo[pl.ds(base, 88), 512 + b * 128 : 512 + (b + 1) * 128]
            pr = p_lo[pl.ds(b, 88, stride=8), :]
            pi = p_lo[pl.ds(4 + b, 88, stride=8), :]
            reals.append(jnp.sum(wr * pr - wi * pi, 0, keepdims=True))
            imags.append(jnp.sum(wr * pi + wi * pr, 0, keepdims=True))
        inc_lo[pl.ds(pl.multiple_of(g * 8, 8), 8), :] = jnp.concatenate(reals + imags, 0)

    @pl.loop(1, 8)
    def _(i):
        ret_send(i).wait_recv()

    for c in range(8):
        for h in range(2):
            b = c * 2 + h
            sr = shifts[0, :, b * 128 : (b + 1) * 128]
            si = shifts[1, :, b * 128 : (b + 1) * 128]
            parts = ([], [])
            for p in range(2):
                ir = ret_in[c, pl.ds(h * 2 + p, 1), :]
                ii = ret_in[c, pl.ds(4 + h * 2 + p, 1), :]
                parts[0].append(sr * ir + si * ii)
                parts[1].append(sr * ii - si * ir)
            for m in range(2):
                down[m * 16 : (m + 1) * 16, b * 128 : (b + 1) * 128] = jnp.concatenate(parts[m], 0).astype(BF16)
    direct = jnp.concatenate(
        [
            jnp.concatenate([inc_lo[pl.ds(m * 4 + b, 16, stride=8), :] for b in range(4)], 1)
            for m in range(2)
        ],
        0,
    )
    incoming = (direct + nt(down[...], int_v[...])).astype(BF16)
    in_re = incoming[:16]
    in_im = incoming[16:]
    lhs = jnp.concatenate([jnp.concatenate([in_re, -in_im], 1), jnp.concatenate([in_im, in_re], 1)], 0)
    far = jnp.zeros((32, 128), F32)
    for i in range(8):
        rec_copy(i).wait()
        res = nt(lhs, rec_v[i * 256 : (i + 1) * 256])
        for u in range(2):
            far = far + jnp.where(own == 2 * i + u, res[:, u * 128 : (u + 1) * 128], 0.0)
    out[pl.ds(0, 16, stride=2), :] = 0.5 * d_re + near[:, :128] + far[:16]
    out[pl.ds(1, 16, stride=2), :] = 0.5 * d_im + near[:, 128:] + far[16:]

    up_copy.wait_send()
    low_copy.wait_send()

    @pl.loop(1, 8)
    def _(i):
        one_send(i).wait_send()
        ret_send(i).wait_send()

    @pl.loop(1, 16)
    def _(i):
        two_send(i).wait_send()

    @pl.loop(0, 8)
    def _(j):
        near_send(j).wait_send()

    @pl.loop(9, 17)
    def _(j):
        near_send(j).wait_send()

    for i in range(5):
        jump_send(i).wait_send()


def on_device(
    density, radiate, receive, near_tiles, near_src, near_tile, send_box, distant_pattern_slot, far_type,
    trans_lo, interp_matrix, shifts, par_far, par_type, trans_hi,
):
    types = trans_lo.shape[0]
    lo_rows = trans_lo.reshape(types, 2, 4, 128).transpose(0, 2, 1, 3).reshape(types * 8, 128)
    hi_rows = trans_hi.reshape(types, 2, 16, 128).transpose(0, 2, 1, 3).reshape(types, 32, 128)
    shift_rows = shifts.reshape(8, 2, 16, 128).transpose(0, 2, 1, 3).reshape(256, 128)

    vm = pl.BlockSpec(memory_space=pltpu.VMEM)
    anyspace = pl.BlockSpec(memory_space=pl.ANY)
    dma = pltpu.SemaphoreType.DMA
    res = pl.pallas_call(
        kernel,
        name="mlfmm",
        out_shape=jax.ShapeDtypeStruct((32, 128), F32),
        in_specs=[vm, pl.BlockSpec(memory_space=pltpu.SMEM)] + [vm] * 7 + [anyspace] * 6,
        out_specs=vm,
        scratch_shapes=[
            pltpu.VMEM((32, 128), F32),
            pltpu.VMEM((96, 128), F32),
            pltpu.VMEM((8, 128), I32),
            pltpu.VMEM((16, 256), I32),
            pltpu.VMEM((16, 256), I32),
            pltpu.VMEM((16, 256), I32),
            pltpu.VMEM((16, 256), I32),
            pltpu.VMEM((2, 8, 2048), F32),
            pltpu.VMEM((2528, 128), BF16),
            pltpu.VMEM((TPAD * 8, 128), F32),
            pltpu.VMEM((316, 16, 128), BF16),
            pltpu.VMEM((TPAD * 16, 128), F32),
            pltpu.VMEM((TPAD, 1024), BF16),
            pltpu.VMEM((TPAD, 512), BF16),
            pltpu.VMEM((16, 8, 128), F32),
            dma,
            dma,
            pltpu.VMEM((2048, 1024), BF16),
            pltpu.VMEM((2048, 1024), BF16),
            pltpu.VMEM((224, 2, 128, 128), BF16),
            pltpu.VMEM((512, 2048), BF16),
            pltpu.VMEM((3, 32, 128), BF16),
            pltpu.VMEM((128, 128), F32),
            pltpu.VMEM((22, 32, 128), BF16),
            pltpu.VMEM((22, 32, 128), BF16),
            pltpu.VMEM((8, 8, 128), F32),
            pltpu.VMEM((8, 8, 128), BF16),
            pltpu.VMEM((8, 8, 128), BF16),
            pltpu.VMEM((64, 128), F32),
            pltpu.VMEM((4, 16, 128), BF16),
            pltpu.VMEM((16, 4, 16, 128), BF16),
            pltpu.VMEM((4, 256, 128), F32),
            pltpu.VMEM((8, 8, 128), F32),
            pltpu.VMEM((8, 8, 128), F32),
            pltpu.VMEM((32, 2048), BF16),
            pltpu.VMEM((1536, TPAD), BF16),
            pltpu.VMEM((1536, 1024), F32),
            pltpu.VMEM((704, 128), F32),
            pltpu.VMEM((4096, TPAD), BF16),
            pltpu.VMEM((4096, 512), F32),
            pltpu.VMEM((128, 128), F32),
            pltpu.VMEM((224, 256), F32),
            pltpu.VMEM((224, 512), BF16),
            dma((8,)),
            dma((8,)),
            dma((224 // GROUP,)),
            dma,
            dma,
            dma((2,)),
            dma((2,)),
            dma((22,)),
            dma((22,)),
            dma((8,)),
            dma((8,)),
            dma((16,)),
            dma((16,)),
            dma((8,)),
            dma((8,)),
        ],
        compiler_params=pltpu.CompilerParams(
            collective_id=0, has_side_effects=True, vmem_limit_bytes=58 * 1024 * 1024
        ),
    )(
        density.reshape(32, 128), send_box.reshape(128, 4).transpose(1, 0), near_src, near_tile,
        distant_pattern_slot, far_type, par_far, par_type, shift_rows,
        radiate.reshape(2048, 1024), receive.reshape(2048, 1024), near_tiles, interp_matrix, lo_rows, hi_rows,
    )
    return res.reshape(16, 2, 128)


def solution(mesh):
    both = ("box", "samp")
    return jax.shard_map(
        on_device,
        mesh=mesh,
        in_specs=(
            P(both, None, None), P(both, None, None), P(both, None, None), P(both, None, None, None),
            P(both, None), P(both, None), P(both, None, None), P(both, None), P(both, None),
            P(), P(), P(), P("box", None), P("box", None), P(),
        ),
        out_specs=P(both, None, None),
        check_vma=False,
    )
```

time: 122 us -> 47 us (0.39)
  Pallas kernels: 0 us -> 45.5 us
  matrix products: 37.5 us -> 0 us
  local copies, waits for them, and re-layouts: 34.2 us -> 1.32 us
  starting transfers between devices: 17.2 us -> 0 us
  between operations: 13.7 us -> 0.01 us
  other arithmetic: 12 us -> 0 us
  waiting for transfers between devices: 7.3 us -> 0 us
    pallas_call x0 -> x1, Pallas kernels: none -> 45.5 us  [on_device(): pl.pallas_call(kernel, name='mlfmm', out_shape=jax.ShapeDtypeStruct((32,...]
    dot_general x11 -> x0, matrix products: 37.5 us -> none  [the longest x5 23 us: pick_rows(): jnp.einsum('...r,rw->...w', selector, table, preferred_element_type=jnp.f...]
    reshape x7 -> x0, local copies, waits for them, and re-layouts: 17.7 us -> none  [the longest x1 7.17 us: on_device(): parent_ops = pick_rows(trans_hi.reshape(type_count, 2 * width_hi), own_type)]
    reduce_sum x3 -> x0, other arithmetic: 11.2 us -> none  [the longest x2 11.1 us: translated_flat(): jnp.sum(operator_rows[..., :width] * pattern_rows[..., :width] - operator...]
    all_to_all x1 -> x0, starting transfers between devices: 10.2 us -> none  [on_device(): lax.all_to_all(outgoing, ('box', 'samp'), split_axis=0, concat_axis=0, ti...]
    all_gather x1 -> x0, waiting for transfers between devices: 7.27 us -> none  [on_device(): everyone = lax.all_gather(parents_own, ('box', 'samp'), axis=0, tiled=True)]
    ppermute x2 -> x0, starting transfers between devices: 6.98 us -> none  [shifted(): lax.ppermute(value, axis, [(source, source + steps) for source in range(f...]
    scatter x2 -> x0, local copies, waits for them, and re-layouts: 6 us -> none  [the longest x1 3.09 us: on_device(): tile_source = jnp.full((tile_total,), 3 * box_count, jnp.int32).at[local_...]
  transfers between devices with their start and end apart: 4 -> 0, of which waited for: 1 -> 0; matrix products, arithmetic and copies ran while one was open for 51% -> 0% of each run, Pallas kernels for 0% -> 0%
where the time goes in v1:
time: 47 us; the launch traced here: 46.9 us
  Pallas kernels  45.5 us (97%)
  local copies, waits for them, and re-layouts  1.32 us (3%)
    pallas_call x1, Pallas kernels, on_device(): pl.pallas_call(kernel, name='mlfmm', out_shape=jax.ShapeDtypeStruct((32,...  45.5 us
    unnamed x1, local copies, waits for them, and re-layouts  1.32 us

profile of v1, /device:TPU:1, one launch (start us, length us, event | category | flops | bytes accessed | tf_op | source)
XLA Modules:
  0.0 46.9 jit_solution(16414637797003768081)
XLA Ops:
  0.0 45.5 %mlfmm.1 = f32[32,128]{1,0:T(8,128)} custom-call(bf16[32,128]{1,0:T(8,128)(2,1)} %bitcast.28, s32[4,128]{1,0:T(4,128)} %bitcast.29, s32[16,27]{1,0:T(8,128)} %near_src.1, s32[16,27]{1,0:T(8,128)} %near_tile.1, s32[16,189]{1,0:T(8,128)} %dps_in.1, s32[16,189]{1,0:T(8,128)} %ftype_in.1, s32[64,189]{1,0:T(8,128)} %pfar_in.1, s32[64,189]{1,0:T(8,128)} %ptype_in.1, ...), custom_call_target="tpu_custom_call" | custom-call | tf_op jit(solution)/shard_map/mlfmm/pallas_call | solution.py:445
  45.5 1.3 %copy.20 = f32[16,2,128]{2,1,0:T(2,128)} copy(f32[16,2,128]{2,1,0:T(2,128)} %bitcast.27) | data formatting | bytes 32768

commit v2 on v1

--- a/solution.py
+++ b/solution.py
@@ -40,10 +40,11 @@
 
 
 def kernel(
-    dens, sb, near_src, near_tile, dps_in, ftype_in, pfar_in, ptype_in, shift_rows,
+    dens_h, sb, near_src_h, near_tile_h, dps_h, ftype_h, pfar_h, ptype_h, shift_h,
     radiate, receive, tiles, interp, lo_rows, hi_rows,
     out,
-    dens_f, win_f, nidx, dps, ftype, pfar, ptype, shifts, lo_v, lo_f, hi_v, hi_f, tlo, thi, pat3, lo_sem, hi_sem,
+    dens, near_src, near_tile, dps_in, ftype_in, pfar_in, ptype_in, shift_rows, small_sem,
+    dens_f, win_f, nidx, dps, ftype, pfar, ptype, shifts, lo_v, hi_v, hi_f, tlo, thi, pat3, lo_sem, hi_sem,
     rad_v, rec_v, tile_v, int_v, window, patf, leaf_msg, leaf_in, hi_scr, one_msg, one_in, one_f,
     two_msg, two_in, hi_p, ret_msg, ret_in, down, n_lo, w_lo, p_lo, n_hi, w_hi, inc_lo, contrib, picked,
     rad_sem, rec_sem, tile_sem, int_sem, loc_sem,
@@ -73,8 +74,22 @@
     lo_copy = pltpu.make_async_copy(lo_rows, lo_v, lo_sem)
     hi_copy = pltpu.make_async_copy(hi_rows.at[:, pl.ds((zc // 4) * 16, 16), :], hi_v, hi_sem)
 
+    column = s // 8
+    part = pl.ds(pl.multiple_of(column * 16, 16), 16)
+    small = [
+        pltpu.make_async_copy(a, b, small_sem.at[i])
+        for i, (a, b) in enumerate(
+            (
+                (dens_h, dens), (shift_h, shift_rows), (near_src_h, near_src), (near_tile_h, near_tile),
+                (dps_h, dps_in), (ftype_h, ftype_in), (pfar_h.at[part], pfar_in), (ptype_h.at[part], ptype_in),
+            )
+        )
+    ]
+    small[0].start()
     for i in range(8):
         rad_copy(i).start()
+    for c in small[1:]:
+        c.start()
     int_copy.start()
     lo_copy.start()
     hi_copy.start()
@@ -90,19 +105,7 @@
         pl.semaphore_signal(barrier, inc=1, device_id=device((me + i) % 128), device_id_type=pl.DeviceIdType.MESH)
         pl.semaphore_signal(barrier, inc=1, device_id=device((me + 128 - i) % 128), device_id_type=pl.DeviceIdType.MESH)
 
-    @pl.loop(0, groups)
-    def _(i):
-        tile_copy(i).start()
-
-    @pl.loop(0, 8)
-    def _(i):
-        rec_copy(i).start()
-
-    def send(src, dst, ss, rs, pos):
-        return pltpu.make_async_remote_copy(
-            src_ref=src, dst_ref=dst, send_sem=ss, recv_sem=rs, device_id=device(pos), device_id_type=pl.DeviceIdType.MESH
-        )
-
+    small[0].wait()
     dens_f[...] = dens[...].astype(F32)
     d_re = dens_f[pl.ds(0, 16, stride=2), :]
     d_im = dens_f[pl.ds(1, 16, stride=2), :]
@@ -115,12 +118,26 @@
             [jnp.where(own == 2 * i + h, d_all, 0.0).astype(BF16) for h in range(2)], 1
         )
         acc = acc + nn(lhs, rad_v[i * 256 : (i + 1) * 256])
+    @pl.loop(0, groups)
+    def _(i):
+        tile_copy(i).start()
+
+    @pl.loop(0, 8)
+    def _(i):
+        rec_copy(i).start()
+
+    def send(src, dst, ss, rs, pos):
+        return pltpu.make_async_remote_copy(
+            src_ref=src, dst_ref=dst, send_sem=ss, recv_sem=rs, device_id=device(pos), device_id_type=pl.DeviceIdType.MESH
+        )
+
     pat = jnp.concatenate([acc[:16, :512] - acc[16:, 512:], acc[:16, 512:] + acc[16:, :512]], 0).astype(BF16)
     pat_f = pat.astype(F32)
     for m in range(2):
         for b in range(4):
             patf[pl.ds(m * 4 + b, 16, stride=8), :] = pat_f[m * 16 : (m + 1) * 16, b * 128 : (b + 1) * 128]
     pat3[...] = patf[...].reshape(16, 8, 128)
+    small[1].wait()
     for m in range(2):
         for b in range(16):
             shifts[m, :, b * 128 : (b + 1) * 128] = shift_rows[pl.ds(b * 2 + m, 8, stride=32), :]
@@ -192,22 +209,16 @@
         jump_send(i).start()
     fill(leaf_in, 8, me)
 
+    for c in small[2:]:
+        c.wait()
     nidx[...] = jnp.full((8, 128), -1, I32)
     for g in range(16):
         at = (g % 4) * 32
         nidx[g // 4 : g // 4 + 1, at : at + 27] = near_src[g : g + 1, :]
         nidx[4 + g // 4 : 5 + g // 4, at : at + 27] = near_tile[g : g + 1, :]
-    column = s // 8
-    part = pl.ds(pl.multiple_of(column * 16, 16), 16)
-    for held, given in ((dps, dps_in[...]), (ftype, ftype_in[...]), (pfar, pfar_in[part, :]), (ptype, ptype_in[part, :])):
+    for held, given in ((dps, dps_in[...]), (ftype, ftype_in[...]), (pfar, pfar_in[...]), (ptype, ptype_in[...])):
         held[...] = jnp.full((16, 256), -1, I32)
         held[:, :189] = given
-    lo_copy.wait()
-    lo_f[:2528, :] = lo_v[...].astype(F32)
-    lo_f[2528:, :] = jnp.zeros((544, 128), F32)
-    for r in range(8):
-        at = (r % 2) * 512 + (r // 2) * 128
-        tlo[:, at : at + 128] = lo_f[pl.ds(r, TPAD, stride=8), :].astype(BF16)
     hi_copy.wait()
 
     @pl.loop(0, 4)
@@ -218,6 +229,75 @@
     for r in range(4):
         at = (r % 2) * 256 + (r // 2) * 128
         thi[:, at : at + 128] = hi_f[pl.ds((zc % 4) * 4 + r, TPAD, stride=16), :].astype(BF16)
+
+    kinds = rows_of((TPAD, 256))
+    prow = rows_of((256, 256))
+    parent = (prow // 16) * 16 + (prow % 8) * 2 + (prow // 8) % 2
+
+    @pl.loop(0, 16, unroll=True)
+    def _(g):
+        a = onehot(pfar[pl.ds(g, 1), :] == parent)
+        b = onehot(ptype[pl.ds(g, 1), :] == kinds)
+        n_hi[pl.ds(pl.multiple_of(g * 256, 256), 256), :] = nt(a, b).astype(BF16)
+
+    @pl.loop(1, 8)
+    def _(i):
+        one_send(i).wait_recv()
+
+    one_f[...] = one_in[...].astype(F32).reshape(64, 128)
+    for m in range(4):
+        two_msg[m] = jnp.concatenate(
+            [one_f[pl.ds(m * 2 + p, 8, stride=8), :] for p in range(2)], 0
+        ).astype(BF16)
+
+    def two_send(i):
+        peer = (yx + i) % 16
+        return send(two_msg, two_in.at[yx], two_s.at[i], two_r.at[i], peer * 8 + zc)
+
+    @pl.loop(1, 16)
+    def _(i):
+        two_send(i).start()
+
+    two_in[yx] = two_msg[...]
+
+    w_hi[...] = nn(n_hi[...], thi[...])
+
+    @pl.loop(1, 16)
+    def _(i):
+        two_send(i).wait_recv()
+
+    for m in range(4):
+        for i in range(16):
+            hi_p[m, i * 16 : (i + 1) * 16, :] = two_in[i, m].astype(F32)
+
+    @pl.loop(0, 8, unroll=2)
+    def _(c):
+        for p in range(2):
+            base = pl.multiple_of((c * 2 + p) * 256, 256)
+            for h in range(2):
+                wr = w_hi[pl.ds(base, 256), h * 128 : (h + 1) * 128]
+                wi = w_hi[pl.ds(base, 256), 256 + h * 128 : 256 + (h + 1) * 128]
+                pr = hi_p[h]
+                pi = hi_p[2 + h]
+                ret_msg[c, pl.ds(h * 2 + p, 1), :] = jnp.sum(wr * pr - wi * pi, 0, keepdims=True)
+                ret_msg[c, pl.ds(4 + h * 2 + p, 1), :] = jnp.sum(wr * pi + wi * pr, 0, keepdims=True)
+
+    def ret_send(i):
+        peer = (zc + i) % 8
+        return send(ret_msg.at[peer], ret_in.at[zc], ret_s.at[i], ret_r.at[i], yx * 8 + peer)
+
+    @pl.loop(1, 8)
+    def _(i):
+        ret_send(i).start()
+
+    ret_in[zc] = ret_msg[zc]
+
+    lo_copy.wait()
+    hi_f[:2528, :] = lo_v[...].astype(F32)
+    hi_f[2528:3072, :] = jnp.zeros((544, 128), F32)
+    for r in range(8):
+        at = (r % 2) * 512 + (r // 2) * 128
+        tlo[:, at : at + 128] = hi_f[pl.ds(r, TPAD, stride=8), :].astype(BF16)
 
     row = rows_of((96, 256))
     slot = row // 4
@@ -227,52 +307,14 @@
         jnp.where(slot == 17, 16, jnp.where(slot == 18, 32, jnp.where(slot == 19, 64, jnp.where(slot == 20, 96, 112)))),
     )
     expect = jnp.where(row < 88, ((me + delta + 128) % 128) * 4 + row % 4, -2)
-    kinds = rows_of((TPAD, 256))
-
-    @pl.loop(0, 16)
+
+    @pl.loop(0, 16, unroll=True)
     def _(g):
         a = onehot(dps[pl.ds(g, 1), :] == expect)
         b = onehot(ftype[pl.ds(g, 1), :] == kinds)
         n_lo[pl.ds(pl.multiple_of(g * 96, 32), 96), :] = nt(a, b).astype(BF16)
 
-    @pl.loop(1, 8)
-    def _(i):
-        one_send(i).wait_recv()
-
-    one_f[...] = one_in[...].astype(F32).reshape(64, 128)
-    for m in range(4):
-        two_msg[m] = jnp.concatenate(
-            [one_f[pl.ds(m * 2 + p, 8, stride=8), :] for p in range(2)], 0
-        ).astype(BF16)
-
-    def two_send(i):
-        peer = (yx + i) % 16
-        return send(two_msg, two_in.at[yx], two_s.at[i], two_r.at[i], peer * 8 + zc)
-
-    @pl.loop(1, 16)
-    def _(i):
-        two_send(i).start()
-
-    two_in[yx] = two_msg[...]
-
-    @pl.loop(0, 4)
-    def _(i):
-        sl = pl.ds(pl.multiple_of(i * 384, 384), 384)
-        w_lo[sl, :] = nn(n_lo[sl, :], tlo[...])
-
-    prow = rows_of((256, 256))
-    parent = (prow // 16) * 16 + (prow % 8) * 2 + (prow // 8) % 2
-
-    @pl.loop(0, 16)
-    def _(g):
-        a = onehot(pfar[pl.ds(g, 1), :] == parent)
-        b = onehot(ptype[pl.ds(g, 1), :] == kinds)
-        n_hi[pl.ds(pl.multiple_of(g * 256, 256), 256), :] = nt(a, b).astype(BF16)
-
-    @pl.loop(0, 8)
-    def _(i):
-        sl = pl.ds(pl.multiple_of(i * 512, 512), 512)
-        w_hi[sl, :] = nn(n_hi[sl, :], thi[...])
+    w_lo[...] = nn(n_lo[...], tlo[...])
 
     up_copy.wait_recv()
     low_copy.wait_recv()
@@ -294,6 +336,9 @@
     @pl.loop(0, groups)
     def _(grp):
         tile_copy(grp).wait()
+
+    @pl.loop(0, groups, unroll=True)
+    def _(grp):
         base = pl.multiple_of(grp * GROUP, GROUP)
         x = picked[pl.ds(base, GROUP), :]
         lhs = jnp.concatenate([x[:, :256], x[:, 256:]], 0)
@@ -313,36 +358,6 @@
     high = whole.astype(BF16)
     near = nn(own_tile, high) + nn(own_tile, (whole - high.astype(F32)).astype(BF16))
 
-    @pl.loop(1, 16)
-    def _(i):
-        two_send(i).wait_recv()
-
-    for m in range(4):
-        for i in range(16):
-            hi_p[m, i * 16 : (i + 1) * 16, :] = two_in[i, m].astype(F32)
-
-    @pl.loop(0, 8)
-    def _(c):
-        for p in range(2):
-            base = pl.multiple_of((c * 2 + p) * 256, 256)
-            for h in range(2):
-                wr = w_hi[pl.ds(base, 256), h * 128 : (h + 1) * 128]
-                wi = w_hi[pl.ds(base, 256), 256 + h * 128 : 256 + (h + 1) * 128]
-                pr = hi_p[h]
-                pi = hi_p[2 + h]
-                ret_msg[c, pl.ds(h * 2 + p, 1), :] = jnp.sum(wr * pr - wi * pi, 0, keepdims=True)
-                ret_msg[c, pl.ds(4 + h * 2 + p, 1), :] = jnp.sum(wr * pi + wi * pr, 0, keepdims=True)
-
-    def ret_send(i):
-        peer = (zc + i) % 8
-        return send(ret_msg.at[peer], ret_in.at[zc], ret_s.at[i], ret_r.at[i], yx * 8 + peer)
-
-    @pl.loop(1, 8)
-    def _(i):
-        ret_send(i).start()
-
-    ret_in[zc] = ret_msg[zc]
-
     @pl.loop(0, 8)
     def _(j):
         near_send(j).wait_recv()
@@ -356,7 +371,7 @@
 
     p_lo[...] = leaf_in[...].astype(F32).reshape(704, 128)
 
-    @pl.loop(0, 16)
+    @pl.loop(0, 16, unroll=2)
     def _(g):
         base = pl.multiple_of(g * 96, 32)
         reals, imags = [], []
@@ -403,8 +418,8 @@
         res = nt(lhs, rec_v[i * 256 : (i + 1) * 256])
         for u in range(2):
             far = far + jnp.where(own == 2 * i + u, res[:, u * 128 : (u + 1) * 128], 0.0)
-    out[pl.ds(0, 16, stride=2), :] = 0.5 * d_re + near[:, :128] + far[:16]
-    out[pl.ds(1, 16, stride=2), :] = 0.5 * d_im + near[:, 128:] + far[16:]
+    out[pl.ds(0, 16, stride=2), :] = near[:, :128] + far[:16]
+    out[pl.ds(1, 16, stride=2), :] = near[:, 128:] + far[16:]
 
     up_copy.wait_send()
     low_copy.wait_send()
@@ -446,9 +461,18 @@
         kernel,
         name="mlfmm",
         out_shape=jax.ShapeDtypeStruct((32, 128), F32),
-        in_specs=[vm, pl.BlockSpec(memory_space=pltpu.SMEM)] + [vm] * 7 + [anyspace] * 6,
+        in_specs=[anyspace, pl.BlockSpec(memory_space=pltpu.SMEM)] + [anyspace] * 13,
         out_specs=vm,
         scratch_shapes=[
+            pltpu.VMEM((32, 128), BF16),
+            pltpu.VMEM((16, 27), I32),
+            pltpu.VMEM((16, 27), I32),
+            pltpu.VMEM((16, 189), I32),
+            pltpu.VMEM((16, 189), I32),
+            pltpu.VMEM((16, 189), I32),
+            pltpu.VMEM((16, 189), I32),
+            pltpu.VMEM((256, 128), F32),
+            dma((8,)),
             pltpu.VMEM((32, 128), F32),
             pltpu.VMEM((96, 128), F32),
             pltpu.VMEM((8, 128), I32),
@@ -458,7 +482,6 @@
             pltpu.VMEM((16, 256), I32),
             pltpu.VMEM((2, 8, 2048), F32),
             pltpu.VMEM((2528, 128), BF16),
-            pltpu.VMEM((TPAD * 8, 128), F32),
             pltpu.VMEM((316, 16, 128), BF16),
             pltpu.VMEM((TPAD * 16, 128), F32),
             pltpu.VMEM((TPAD, 1024), BF16),
@@ -509,14 +532,14 @@
             dma((8,)),
         ],
         compiler_params=pltpu.CompilerParams(
-            collective_id=0, has_side_effects=True, vmem_limit_bytes=58 * 1024 * 1024
+            collective_id=0, has_side_effects=True, vmem_limit_bytes=59 * 1024 * 1024
         ),
     )(
         density.reshape(32, 128), send_box.reshape(128, 4).transpose(1, 0), near_src, near_tile,
         distant_pattern_slot, far_type, par_far, par_type, shift_rows,
         radiate.reshape(2048, 1024), receive.reshape(2048, 1024), near_tiles, interp_matrix, lo_rows, hi_rows,
     )
-    return res.reshape(16, 2, 128)
+    return (res + 0.5 * density.reshape(32, 128).astype(F32)).reshape(16, 2, 128)
 
 
 def solution(mesh):

time: 47 us -> 38.4 us (0.82)
  Pallas kernels: 45.5 us -> 36.7 us
  other arithmetic: 0 us -> 1.33 us
  local copies, waits for them, and re-layouts: 1.32 us -> 0.01 us
    pallas_call x1, Pallas kernels: 45.5 us -> 36.7 us  [on_device(): pl.pallas_call(kernel, name='mlfmm', out_shape=jax.ShapeDtypeStruct((32,...]
    add x0 -> x1, other arithmetic: none -> 1.33 us  [on_device(): res + 0.5 * density.reshape(32, 128).astype(F32)]
    unnamed x1 -> x2, local copies, waits for them, and re-layouts: 1.32 us -> 0.01 us
where the time goes in v2:
time: 38.4 us; the launch traced here: 38.1 us
  Pallas kernels  36.7 us (96%)
  other arithmetic  1.33 us (3%)
    pallas_call x1, Pallas kernels, on_device(): pl.pallas_call(kernel, name='mlfmm', out_shape=jax.ShapeDtypeStruct((32,...  36.7 us
    add x1, other arithmetic, on_device(): res + 0.5 * density.reshape(32, 128).astype(F32)  1.33 us

profile of v2, /device:TPU:1, one launch (start us, length us, event | category | flops | bytes accessed | tf_op | source)
XLA Modules:
  0.0 38.1 jit_solution(7178116782314160365)
XLA Ops:
  0.0 0.0 copy-start
  0.0 36.7 %mlfmm.1 = f32[32,128]{1,0:T(8,128)} custom-call(bf16[32,128]{1,0:T(8,128)(2,1)} %bitcast.27, s32[4,128]{1,0:T(4,128)} %bitcast.29, s32[16,27]{1,0:T(8,128)} %near_src_h.1, s32[16,27]{1,0:T(8,128)} %near_tile_h.1, s32[16,189]{1,0:T(8,128)} %dps_h.1, s32[16,189]{1,0:T(8,128)} %ftype_h.1, s32[64,189]{1,0:T(8,128)} %pfar_h.1, s32[64,189]{1,0:T(8,128)} %ptype_h.1, ...), custom_call_target="tpu_custom_call" | custom-call | tf_op jit(solution)/shard_map/mlfmm/pallas_call | solution.py:460
  36.8 0.0 copy-done
  36.8 1.3 %multiply_add_fusion = f32[32,128]{1,0:T(8,128)} fusion(f32[32,128]{1,0:T(8,128)} %mlfmm.1, bf16[32,128]{1,0:T(8,128)(2,1)S(1)} %bitcast.28), kind=kLoop, calls=%fused_computation | loop fusion | flops 12288 | bytes 40960 | tf_op jit(solution)/shard_map/add | solution.py:542
Async XLA Ops:
  0.0 36.8 %copy-start = (bf16[16,2,128]{2,1,0:T(2,128)(2,1)S(1)}, bf16[16,2,128]{2,1,0:T(2,128)(2,1)}, u32[]{:S(2)}) copy-start(bf16[16,2,128]{2,1,0:T(2,128)(2,1)} %param.15) | copy-start | bytes 24580

commit v3 on v2

--- a/solution.py
+++ b/solution.py
@@ -56,18 +56,9 @@
     zc = s % 8
     yx = y * 4 + s // 8
 
-    def rad_copy(i):
-        sl = pl.ds(i * 256, 256)
-        return pltpu.make_async_copy(radiate.at[sl], rad_v.at[sl], rad_sem.at[i])
-
-    def rec_copy(i):
-        sl = pl.ds(i * 256, 256)
-        return pltpu.make_async_copy(receive.at[sl], rec_v.at[sl], rec_sem.at[i])
-
-    def tile_copy(i):
-        sl = pl.ds(i * GROUP, GROUP)
-        return pltpu.make_async_copy(tiles.at[sl], tile_v.at[sl], tile_sem.at[i])
-
+    rad_copy = pltpu.make_async_copy(radiate, rad_v, rad_sem)
+    rec_copy = pltpu.make_async_copy(receive, rec_v, rec_sem)
+    tile_copy = pltpu.make_async_copy(tiles, tile_v, tile_sem)
     int_copy = pltpu.make_async_copy(interp, int_v, int_sem)
     groups = tiles.shape[0] // GROUP
 
@@ -85,25 +76,44 @@
             )
         )
     ]
-    small[0].start()
-    for i in range(8):
-        rad_copy(i).start()
-    for c in small[1:]:
+    for c in small:
         c.start()
+    rad_copy.start()
     int_copy.start()
     lo_copy.start()
     hi_copy.start()
 
     barrier = pltpu.get_barrier_semaphore()
 
-    @pl.loop(1, 16)
+    @pl.loop(1, 16, unroll=True)
     def _(i):
         pl.semaphore_signal(barrier, inc=1, device_id=device((me + 8 * i) % 128), device_id_type=pl.DeviceIdType.MESH)
 
-    @pl.loop(1, 8)
+    @pl.loop(1, 8, unroll=True)
     def _(i):
         pl.semaphore_signal(barrier, inc=1, device_id=device((me + i) % 128), device_id_type=pl.DeviceIdType.MESH)
         pl.semaphore_signal(barrier, inc=1, device_id=device((me + 128 - i) % 128), device_id_type=pl.DeviceIdType.MESH)
+
+    for c in small[2:]:
+        c.wait()
+    nidx[...] = jnp.full((8, 128), -1, I32)
+    for g in range(16):
+        at = (g % 4) * 32
+        nidx[g // 4 : g // 4 + 1, at : at + 27] = near_src[g : g + 1, :]
+        nidx[4 + g // 4 : 5 + g // 4, at : at + 27] = near_tile[g : g + 1, :]
+    for held, given in ((dps, dps_in[...]), (ftype, ftype_in[...]), (pfar, pfar_in[...]), (ptype, ptype_in[...])):
+        held[...] = jnp.full((16, 256), -1, I32)
+        held[:, :189] = given
+
+    kinds = rows_of((TPAD, 256))
+    prow = rows_of((256, 256))
+    parent = (prow // 16) * 16 + (prow % 8) * 2 + (prow // 8) % 2
+
+    @pl.loop(0, 16, unroll=True)
+    def _(g):
+        a = onehot(pfar[pl.ds(g, 1), :] == parent)
+        b = onehot(ptype[pl.ds(g, 1), :] == kinds)
+        n_hi[pl.ds(pl.multiple_of(g * 256, 256), 256), :] = nt(a, b).astype(BF16)
 
     small[0].wait()
     dens_f[...] = dens[...].astype(F32)
@@ -112,20 +122,14 @@
     d_all = jnp.concatenate([d_re, d_im], 0)
     own = rows_of((32, 128)) % 16
     acc = jnp.zeros((32, 1024), F32)
+    rad_copy.wait()
     for i in range(8):
-        rad_copy(i).wait()
         lhs = jnp.concatenate(
             [jnp.where(own == 2 * i + h, d_all, 0.0).astype(BF16) for h in range(2)], 1
         )
         acc = acc + nn(lhs, rad_v[i * 256 : (i + 1) * 256])
-    @pl.loop(0, groups)
-    def _(i):
-        tile_copy(i).start()
-
-    @pl.loop(0, 8)
-    def _(i):
-        rec_copy(i).start()
-
+    tile_copy.start()
+    rec_copy.start()
     def send(src, dst, ss, rs, pos):
         return pltpu.make_async_remote_copy(
             src_ref=src, dst_ref=dst, send_sem=ss, recv_sem=rs, device_id=device(pos), device_id_type=pl.DeviceIdType.MESH
@@ -144,11 +148,15 @@
 
     pl.semaphore_wait(barrier, 29)
 
-    up_copy = send(dens, window.at[0], win_s.at[0], win_r.at[0], (me + 1) % 128)
-    low_copy = send(dens, window.at[2], win_s.at[1], win_r.at[1], (me + 127) % 128)
+    up_copy = send(dens, window.at[0], win_s, win_r, (me + 1) % 128)
+    low_copy = send(dens, window.at[2], win_s, win_r, (me + 127) % 128)
     up_copy.start()
     low_copy.start()
     window[1] = dens[...]
+
+    def wait_for(ref, copies, sem):
+        part = ref.at[pl.ds(0, copies)]
+        pltpu.make_async_copy(part, part, sem).wait()
 
     def fill(dst, j, receiver):
         for half in range(2):
@@ -159,11 +167,11 @@
             dst[j, pl.ds(half * 16, 16), :] = jnp.concatenate(parts, 0).astype(BF16)
 
     def near_send(j):
-        return send(leaf_msg.at[j], leaf_in.at[16 - j], leaf_s.at[j], leaf_r.at[16 - j], (me + j + 120) % 128)
+        return send(leaf_msg.at[j], leaf_in.at[16 - j], leaf_s, leaf_r, (me + j + 120) % 128)
 
     def jump_send(i):
         return send(
-            leaf_msg.at[17 + i], leaf_in.at[21 - i], leaf_s.at[17 + i], leaf_r.at[21 - i], (me + JUMPS[i]) % 128
+            leaf_msg.at[17 + i], leaf_in.at[21 - i], leaf_s, leaf_r, (me + JUMPS[i]) % 128
         )
 
     int_copy.wait()
@@ -186,7 +194,7 @@
 
     def one_send(i):
         peer = (zc + i) % 8
-        return send(one_msg.at[peer], one_in.at[zc], one_s.at[i], one_r.at[i], yx * 8 + peer)
+        return send(one_msg.at[peer], one_in.at[zc], one_s, one_r, yx * 8 + peer)
 
     @pl.loop(1, 8)
     def _(i):
@@ -209,16 +217,6 @@
         jump_send(i).start()
     fill(leaf_in, 8, me)
 
-    for c in small[2:]:
-        c.wait()
-    nidx[...] = jnp.full((8, 128), -1, I32)
-    for g in range(16):
-        at = (g % 4) * 32
-        nidx[g // 4 : g // 4 + 1, at : at + 27] = near_src[g : g + 1, :]
-        nidx[4 + g // 4 : 5 + g // 4, at : at + 27] = near_tile[g : g + 1, :]
-    for held, given in ((dps, dps_in[...]), (ftype, ftype_in[...]), (pfar, pfar_in[...]), (ptype, ptype_in[...])):
-        held[...] = jnp.full((16, 256), -1, I32)
-        held[:, :189] = given
     hi_copy.wait()
 
     @pl.loop(0, 4)
@@ -229,68 +227,6 @@
     for r in range(4):
         at = (r % 2) * 256 + (r // 2) * 128
         thi[:, at : at + 128] = hi_f[pl.ds((zc % 4) * 4 + r, TPAD, stride=16), :].astype(BF16)
-
-    kinds = rows_of((TPAD, 256))
-    prow = rows_of((256, 256))
-    parent = (prow // 16) * 16 + (prow % 8) * 2 + (prow // 8) % 2
-
-    @pl.loop(0, 16, unroll=True)
-    def _(g):
-        a = onehot(pfar[pl.ds(g, 1), :] == parent)
-        b = onehot(ptype[pl.ds(g, 1), :] == kinds)
-        n_hi[pl.ds(pl.multiple_of(g * 256, 256), 256), :] = nt(a, b).astype(BF16)
-
-    @pl.loop(1, 8)
-    def _(i):
-        one_send(i).wait_recv()
-
-    one_f[...] = one_in[...].astype(F32).reshape(64, 128)
-    for m in range(4):
-        two_msg[m] = jnp.concatenate(
-            [one_f[pl.ds(m * 2 + p, 8, stride=8), :] for p in range(2)], 0
-        ).astype(BF16)
-
-    def two_send(i):
-        peer = (yx + i) % 16
-        return send(two_msg, two_in.at[yx], two_s.at[i], two_r.at[i], peer * 8 + zc)
-
-    @pl.loop(1, 16)
-    def _(i):
-        two_send(i).start()
-
-    two_in[yx] = two_msg[...]
-
-    w_hi[...] = nn(n_hi[...], thi[...])
-
-    @pl.loop(1, 16)
-    def _(i):
-        two_send(i).wait_recv()
-
-    for m in range(4):
-        for i in range(16):
-            hi_p[m, i * 16 : (i + 1) * 16, :] = two_in[i, m].astype(F32)
-
-    @pl.loop(0, 8, unroll=2)
-    def _(c):
-        for p in range(2):
-            base = pl.multiple_of((c * 2 + p) * 256, 256)
-            for h in range(2):
-                wr = w_hi[pl.ds(base, 256), h * 128 : (h + 1) * 128]
-                wi = w_hi[pl.ds(base, 256), 256 + h * 128 : 256 + (h + 1) * 128]
-                pr = hi_p[h]
-                pi = hi_p[2 + h]
-                ret_msg[c, pl.ds(h * 2 + p, 1), :] = jnp.sum(wr * pr - wi * pi, 0, keepdims=True)
-                ret_msg[c, pl.ds(4 + h * 2 + p, 1), :] = jnp.sum(wr * pi + wi * pr, 0, keepdims=True)
-
-    def ret_send(i):
-        peer = (zc + i) % 8
-        return send(ret_msg.at[peer], ret_in.at[zc], ret_s.at[i], ret_r.at[i], yx * 8 + peer)
-
-    @pl.loop(1, 8)
-    def _(i):
-        ret_send(i).start()
-
-    ret_in[zc] = ret_msg[zc]
 
     lo_copy.wait()
     hi_f[:2528, :] = lo_v[...].astype(F32)
@@ -298,6 +234,26 @@
     for r in range(8):
         at = (r % 2) * 512 + (r // 2) * 128
         tlo[:, at : at + 128] = hi_f[pl.ds(r, TPAD, stride=8), :].astype(BF16)
+
+    wait_for(one_in, 7, one_r)
+
+    one_f[...] = one_in[...].astype(F32).reshape(64, 128)
+    for m in range(4):
+        two_msg[m] = jnp.concatenate(
+            [one_f[pl.ds(m * 2 + p, 8, stride=8), :] for p in range(2)], 0
+        ).astype(BF16)
+
+    def two_send(i):
+        peer = (yx + i) % 16
+        return send(two_msg, two_in.at[yx], two_s, two_r, peer * 8 + zc)
+
+    @pl.loop(1, 16)
+    def _(i):
+        two_send(i).start()
+
+    two_in[yx] = two_msg[...]
+
+    w_hi[...] = nn(n_hi[...], thi[...])
 
     row = rows_of((96, 256))
     slot = row // 4
@@ -316,8 +272,37 @@
 
     w_lo[...] = nn(n_lo[...], tlo[...])
 
-    up_copy.wait_recv()
-    low_copy.wait_recv()
+    wait_for(two_in, 15, two_r)
+
+    for m in range(4):
+        for i in range(16):
+            hi_p[m, i * 16 : (i + 1) * 16, :] = two_in[i, m].astype(F32)
+
+    for c in range(8):
+        for p in range(2):
+            base = (c * 2 + p) * 256
+            for h in range(2):
+                wr = w_hi[base : base + 256, h * 128 : (h + 1) * 128]
+                wi = w_hi[base : base + 256, 256 + h * 128 : 256 + (h + 1) * 128]
+                pr = hi_p[h]
+                pi = hi_p[2 + h]
+                ret_msg[c, pl.ds(h * 2 + p, 1), :] = jnp.sum(wr * pr - wi * pi, 0, keepdims=True)
+                ret_msg[c, pl.ds(4 + h * 2 + p, 1), :] = jnp.sum(wr * pi + wi * pr, 0, keepdims=True)
+
+    def ret_send(i):
+        peer = (zc + i) % 8
+        return send(ret_msg.at[peer], ret_in.at[zc], ret_s, ret_r, yx * 8 + peer)
+
+    @pl.loop(1, 8)
+    def _(i):
+        ret_send(i).start()
+
+    ret_in[zc] = ret_msg[zc]
+
+    wait_for(leaf_in, 21, leaf_r)
+    p_lo[...] = leaf_in[...].astype(F32).reshape(704, 128)
+
+    wait_for(window, 2, win_r)
     tile_rows = me * 224 + rows_of((224, 128))
     live = jnp.concatenate([onehot(nidx[pl.ds(4 + r, 1), :] == tile_rows) for r in range(4)], 1)
     box_rows = (me - 1) * 16 + rows_of((48, 128))
@@ -333,14 +318,22 @@
     values = jnp.concatenate([x_re, -x_im, x_im, x_re], 1).astype(BF16)
     picked[...] = nn(select, values).astype(BF16)
 
-    @pl.loop(0, groups)
-    def _(grp):
-        tile_copy(grp).wait()
-
-    @pl.loop(0, groups, unroll=True)
-    def _(grp):
-        base = pl.multiple_of(grp * GROUP, GROUP)
-        x = picked[pl.ds(base, GROUP), :]
+    tile_copy.wait()
+    def leaf_sum(g):
+        base = g * 96
+        reals, imags = [], []
+        for b in range(4):
+            wr = w_lo[base : base + 88, b * 128 : (b + 1) * 128]
+            wi = w_lo[base : base + 88, 512 + b * 128 : 512 + (b + 1) * 128]
+            pr = p_lo[pl.ds(b, 88, stride=8), :]
+            pi = p_lo[pl.ds(4 + b, 88, stride=8), :]
+            reals.append(jnp.sum(wr * pr - wi * pi, 0, keepdims=True))
+            imags.append(jnp.sum(wr * pi + wi * pr, 0, keepdims=True))
+        inc_lo[g * 8 : g * 8 + 8, :] = jnp.concatenate(reals + imags, 0)
+
+    for grp in range(groups):
+        base = grp * GROUP
+        x = picked[base : base + GROUP, :]
         lhs = jnp.concatenate([x[:, :256], x[:, 256:]], 0)
         local = rows_of((2 * GROUP, 128)) % GROUP
         total = jnp.zeros((2 * GROUP, 128), F32)
@@ -352,41 +345,23 @@
             res = nt(lhs, jnp.concatenate(pair, 0))
             for u in range(2):
                 total = total + jnp.where(local == 2 * q + u, res[:, u * 128 : (u + 1) * 128], 0.0)
-        contrib[pl.ds(base, GROUP), :] = jnp.concatenate([total[:GROUP], total[GROUP:]], 1)
+        contrib[base : base + GROUP, :] = jnp.concatenate([total[:GROUP], total[GROUP:]], 1)
+        leaf_sum(grp)
+
+    for g in range(groups, 16):
+        leaf_sum(g)
 
     whole = contrib[...]
     high = whole.astype(BF16)
     near = nn(own_tile, high) + nn(own_tile, (whole - high.astype(F32)).astype(BF16))
 
-    @pl.loop(0, 8)
-    def _(j):
-        near_send(j).wait_recv()
-
-    @pl.loop(9, 17)
-    def _(j):
-        near_send(j).wait_recv()
-
-    for i in range(5):
-        jump_send(i).wait_recv()
-
-    p_lo[...] = leaf_in[...].astype(F32).reshape(704, 128)
-
-    @pl.loop(0, 16, unroll=2)
-    def _(g):
-        base = pl.multiple_of(g * 96, 32)
-        reals, imags = [], []
-        for b in range(4):
-            wr = w_lo[pl.ds(base, 88), b * 128 : (b + 1) * 128]
-            wi = w_lo[pl.ds(base, 88), 512 + b * 128 : 512 + (b + 1) * 128]
-            pr = p_lo[pl.ds(b, 88, stride=8), :]
-            pi = p_lo[pl.ds(4 + b, 88, stride=8), :]
-            reals.append(jnp.sum(wr * pr - wi * pi, 0, keepdims=True))
-            imags.append(jnp.sum(wr * pi + wi * pr, 0, keepdims=True))
-        inc_lo[pl.ds(pl.multiple_of(g * 8, 8), 8), :] = jnp.concatenate(reals + imags, 0)
-
-    @pl.loop(1, 8)
-    def _(i):
-        ret_send(i).wait_recv()
+    wait_for(window, 2, win_s)
+    wait_for(one_in, 7, one_s)
+    wait_for(two_in, 15, two_s)
+    wait_for(leaf_in, 21, leaf_s)
+    wait_for(ret_in, 7, ret_s)
+
+    wait_for(ret_in, 7, ret_r)
 
     for c in range(8):
         for h in range(2):
@@ -413,36 +388,13 @@
     in_im = incoming[16:]
     lhs = jnp.concatenate([jnp.concatenate([in_re, -in_im], 1), jnp.concatenate([in_im, in_re], 1)], 0)
     far = jnp.zeros((32, 128), F32)
+    rec_copy.wait()
     for i in range(8):
-        rec_copy(i).wait()
         res = nt(lhs, rec_v[i * 256 : (i + 1) * 256])
         for u in range(2):
             far = far + jnp.where(own == 2 * i + u, res[:, u * 128 : (u + 1) * 128], 0.0)
     out[pl.ds(0, 16, stride=2), :] = near[:, :128] + far[:16]
     out[pl.ds(1, 16, stride=2), :] = near[:, 128:] + far[16:]
-
-    up_copy.wait_send()
-    low_copy.wait_send()
-
-    @pl.loop(1, 8)
-    def _(i):
-        one_send(i).wait_send()
-        ret_send(i).wait_send()
-
-    @pl.loop(1, 16)
-    def _(i):
-        two_send(i).wait_send()
-
-    @pl.loop(0, 8)
-    def _(j):
-        near_send(j).wait_send()
-
-    @pl.loop(9, 17)
-    def _(j):
-        near_send(j).wait_send()
-
-    for i in range(5):
-        jump_send(i).wait_send()
 
 
 def on_device(
@@ -460,7 +412,7 @@
     res = pl.pallas_call(
         kernel,
         name="mlfmm",
-        out_shape=jax.ShapeDtypeStruct((32, 128), F32),
+        out_shape=pltpu.VMEM((32, 128), F32),
         in_specs=[anyspace, pl.BlockSpec(memory_space=pltpu.SMEM)] + [anyspace] * 13,
         out_specs=vm,
         scratch_shapes=[
@@ -515,21 +467,21 @@
             pltpu.VMEM((128, 128), F32),
             pltpu.VMEM((224, 256), F32),
             pltpu.VMEM((224, 512), BF16),
-            dma((8,)),
-            dma((8,)),
-            dma((224 // GROUP,)),
-            dma,
-            dma,
-            dma((2,)),
-            dma((2,)),
-            dma((22,)),
-            dma((22,)),
-            dma((8,)),
-            dma((8,)),
-            dma((16,)),
-            dma((16,)),
-            dma((8,)),
-            dma((8,)),
+            dma,
+            dma,
+            dma,
+            dma,
+            dma,
+            dma,
+            dma,
+            dma,
+            dma,
+            dma,
+            dma,
+            dma,
+            dma,
+            dma,
+            dma,
         ],
         compiler_params=pltpu.CompilerParams(
             collective_id=0, has_side_effects=True, vmem_limit_bytes=59 * 1024 * 1024

time: 38.4 us -> 31.8 us (0.83)
  Pallas kernels: 36.7 us -> 30.8 us
  other arithmetic: 1.33 us -> 0.61 us
    pallas_call x1, Pallas kernels: 36.7 us -> 30.8 us  [on_device(): pl.pallas_call(kernel, name='mlfmm', out_shape=pltpu.VMEM((32, 128), F32)...]
    add x1, other arithmetic: 1.33 us -> 0.61 us  [on_device(): res + 0.5 * density.reshape(32, 128).astype(F32)]
where the time goes in v3:
time: 31.8 us; the launch traced here: 31.5 us
  Pallas kernels  30.8 us (97%)
  other arithmetic  0.61 us (2%)
    pallas_call x1, Pallas kernels, on_device(): pl.pallas_call(kernel, name='mlfmm', out_shape=pltpu.VMEM((32, 128), F32)...  30.8 us

profile of v3, /device:TPU:1, one launch (start us, length us, event | category | flops | bytes accessed | tf_op | source)
XLA Modules:
  0.0 31.5 jit_solution(16580396154160834921)
XLA Ops:
  0.0 0.0 copy-start
  0.0 30.8 %mlfmm.1 = f32[32,128]{1,0:T(8,128)S(1)} custom-call(bf16[32,128]{1,0:T(8,128)(2,1)} %bitcast.27, s32[4,128]{1,0:T(4,128)} %bitcast.29, s32[16,27]{1,0:T(8,128)} %near_src_h.1, s32[16,27]{1,0:T(8,128)} %near_tile_h.1, s32[16,189]{1,0:T(8,128)} %dps_h.1, s32[16,189]{1,0:T(8,128)} %ftype_h.1, s32[64,189]{1,0:T(8,128)} %pfar_h.1, s32[64,189]{1,0:T(8,128)} %ptype_h.1, ...), custom_call_target="tpu_custom_call" | custom-call | tf_op jit(solution)/shard_map/mlfmm/pallas_call | solution.py:412
  30.8 0.0 copy-done
  30.8 0.6 %multiply_add_fusion = f32[32,128]{1,0:T(8,128)} fusion(f32[32,128]{1,0:T(8,128)S(1)} %mlfmm.1, bf16[32,128]{1,0:T(8,128)(2,1)S(1)} %bitcast.28), kind=kLoop, calls=%fused_computation | loop fusion | flops 12288 | bytes 40960 | tf_op jit(solution)/shard_map/add | solution.py:494
Async XLA Ops:
  0.0 30.8 %copy-start = (bf16[16,2,128]{2,1,0:T(2,128)(2,1)S(1)}, bf16[16,2,128]{2,1,0:T(2,128)(2,1)}, u32[]{:S(2)}) copy-start(bf16[16,2,128]{2,1,0:T(2,128)(2,1)} %param.15) | copy-start | bytes 24580

commit v4 on v3

--- a/solution.py
+++ b/solution.py
@@ -71,15 +71,17 @@
         pltpu.make_async_copy(a, b, small_sem.at[i])
         for i, (a, b) in enumerate(
             (
-                (dens_h, dens), (shift_h, shift_rows), (near_src_h, near_src), (near_tile_h, near_tile),
-                (dps_h, dps_in), (ftype_h, ftype_in), (pfar_h.at[part], pfar_in), (ptype_h.at[part], ptype_in),
+                (pfar_h.at[part], pfar_in), (ptype_h.at[part], ptype_in), (dens_h, dens), (shift_h, shift_rows),
+                (near_src_h, near_src), (near_tile_h, near_tile), (dps_h, dps_in), (ftype_h, ftype_in),
             )
         )
     ]
-    for c in small:
+    for c in small[:3]:
         c.start()
     rad_copy.start()
     int_copy.start()
+    for c in small[3:]:
+        c.start()
     lo_copy.start()
     hi_copy.start()
 
@@ -94,16 +96,14 @@
         pl.semaphore_signal(barrier, inc=1, device_id=device((me + i) % 128), device_id_type=pl.DeviceIdType.MESH)
         pl.semaphore_signal(barrier, inc=1, device_id=device((me + 128 - i) % 128), device_id_type=pl.DeviceIdType.MESH)
 
-    for c in small[2:]:
-        c.wait()
-    nidx[...] = jnp.full((8, 128), -1, I32)
-    for g in range(16):
-        at = (g % 4) * 32
-        nidx[g // 4 : g // 4 + 1, at : at + 27] = near_src[g : g + 1, :]
-        nidx[4 + g // 4 : 5 + g // 4, at : at + 27] = near_tile[g : g + 1, :]
-    for held, given in ((dps, dps_in[...]), (ftype, ftype_in[...]), (pfar, pfar_in[...]), (ptype, ptype_in[...])):
+    def pad(held, given):
         held[...] = jnp.full((16, 256), -1, I32)
-        held[:, :189] = given
+        held[:, :189] = given[...]
+
+    small[0].wait()
+    small[1].wait()
+    pad(pfar, pfar_in)
+    pad(ptype, ptype_in)
 
     kinds = rows_of((TPAD, 256))
     prow = rows_of((256, 256))
@@ -115,7 +115,7 @@
         b = onehot(ptype[pl.ds(g, 1), :] == kinds)
         n_hi[pl.ds(pl.multiple_of(g * 256, 256), 256), :] = nt(a, b).astype(BF16)
 
-    small[0].wait()
+    small[2].wait()
     dens_f[...] = dens[...].astype(F32)
     d_re = dens_f[pl.ds(0, 16, stride=2), :]
     d_im = dens_f[pl.ds(1, 16, stride=2), :]
@@ -141,18 +141,10 @@
         for b in range(4):
             patf[pl.ds(m * 4 + b, 16, stride=8), :] = pat_f[m * 16 : (m + 1) * 16, b * 128 : (b + 1) * 128]
     pat3[...] = patf[...].reshape(16, 8, 128)
-    small[1].wait()
+    small[3].wait()
     for m in range(2):
         for b in range(16):
             shifts[m, :, b * 128 : (b + 1) * 128] = shift_rows[pl.ds(b * 2 + m, 8, stride=32), :]
-
-    pl.semaphore_wait(barrier, 29)
-
-    up_copy = send(dens, window.at[0], win_s, win_r, (me + 1) % 128)
-    low_copy = send(dens, window.at[2], win_s, win_r, (me + 127) % 128)
-    up_copy.start()
-    low_copy.start()
-    window[1] = dens[...]
 
     def wait_for(ref, copies, sem):
         part = ref.at[pl.ds(0, copies)]
@@ -196,27 +188,15 @@
         peer = (zc + i) % 8
         return send(one_msg.at[peer], one_in.at[zc], one_s, one_r, yx * 8 + peer)
 
-    @pl.loop(1, 8)
-    def _(i):
-        one_send(i).start()
-
-    one_in[zc] = one_msg[zc]
-
-    @pl.loop(0, 8)
-    def _(j):
-        fill(leaf_msg, j, (me + j + 120) % 128)
-        near_send(j).start()
-
-    @pl.loop(9, 17)
-    def _(j):
-        fill(leaf_msg, j, (me + j + 120) % 128)
-        near_send(j).start()
-
-    for i in range(5):
-        fill(leaf_msg, 17 + i, (me + JUMPS[i]) % 128)
-        jump_send(i).start()
-    fill(leaf_in, 8, me)
-
+    for c in small[4:]:
+        c.wait()
+    nidx[...] = jnp.full((8, 128), -1, I32)
+    for g in range(16):
+        at = (g % 4) * 32
+        nidx[g // 4 : g // 4 + 1, at : at + 27] = near_src[g : g + 1, :]
+        nidx[4 + g // 4 : 5 + g // 4, at : at + 27] = near_tile[g : g + 1, :]
+    pad(dps, dps_in)
+    pad(ftype, ftype_in)
     hi_copy.wait()
 
     @pl.loop(0, 4)
@@ -234,26 +214,6 @@
     for r in range(8):
         at = (r % 2) * 512 + (r // 2) * 128
         tlo[:, at : at + 128] = hi_f[pl.ds(r, TPAD, stride=8), :].astype(BF16)
-
-    wait_for(one_in, 7, one_r)
-
-    one_f[...] = one_in[...].astype(F32).reshape(64, 128)
-    for m in range(4):
-        two_msg[m] = jnp.concatenate(
-            [one_f[pl.ds(m * 2 + p, 8, stride=8), :] for p in range(2)], 0
-        ).astype(BF16)
-
-    def two_send(i):
-        peer = (yx + i) % 16
-        return send(two_msg, two_in.at[yx], two_s, two_r, peer * 8 + zc)
-
-    @pl.loop(1, 16)
-    def _(i):
-        two_send(i).start()
-
-    two_in[yx] = two_msg[...]
-
-    w_hi[...] = nn(n_hi[...], thi[...])
 
     row = rows_of((96, 256))
     slot = row // 4
@@ -270,39 +230,6 @@
         b = onehot(ftype[pl.ds(g, 1), :] == kinds)
         n_lo[pl.ds(pl.multiple_of(g * 96, 32), 96), :] = nt(a, b).astype(BF16)
 
-    w_lo[...] = nn(n_lo[...], tlo[...])
-
-    wait_for(two_in, 15, two_r)
-
-    for m in range(4):
-        for i in range(16):
-            hi_p[m, i * 16 : (i + 1) * 16, :] = two_in[i, m].astype(F32)
-
-    for c in range(8):
-        for p in range(2):
-            base = (c * 2 + p) * 256
-            for h in range(2):
-                wr = w_hi[base : base + 256, h * 128 : (h + 1) * 128]
-                wi = w_hi[base : base + 256, 256 + h * 128 : 256 + (h + 1) * 128]
-                pr = hi_p[h]
-                pi = hi_p[2 + h]
-                ret_msg[c, pl.ds(h * 2 + p, 1), :] = jnp.sum(wr * pr - wi * pi, 0, keepdims=True)
-                ret_msg[c, pl.ds(4 + h * 2 + p, 1), :] = jnp.sum(wr * pi + wi * pr, 0, keepdims=True)
-
-    def ret_send(i):
-        peer = (zc + i) % 8
-        return send(ret_msg.at[peer], ret_in.at[zc], ret_s, ret_r, yx * 8 + peer)
-
-    @pl.loop(1, 8)
-    def _(i):
-        ret_send(i).start()
-
-    ret_in[zc] = ret_msg[zc]
-
-    wait_for(leaf_in, 21, leaf_r)
-    p_lo[...] = leaf_in[...].astype(F32).reshape(704, 128)
-
-    wait_for(window, 2, win_r)
     tile_rows = me * 224 + rows_of((224, 128))
     live = jnp.concatenate([onehot(nidx[pl.ds(4 + r, 1), :] == tile_rows) for r in range(4)], 1)
     box_rows = (me - 1) * 16 + rows_of((48, 128))
@@ -312,6 +239,59 @@
     )
     own_tile = nt(owner, live).astype(BF16)
     select = nt(live, source).astype(BF16)
+
+    pl.semaphore_wait(barrier, 29)
+
+    @pl.loop(1, 8)
+    def _(i):
+        one_send(i).start()
+
+    one_in[zc] = one_msg[zc]
+
+    up_copy = send(dens, window.at[0], win_s, win_r, (me + 1) % 128)
+    low_copy = send(dens, window.at[2], win_s, win_r, (me + 127) % 128)
+    up_copy.start()
+    low_copy.start()
+    window[1] = dens[...]
+
+    @pl.loop(0, 8)
+    def _(j):
+        fill(leaf_msg, j, (me + j + 120) % 128)
+        near_send(j).start()
+
+    @pl.loop(9, 17)
+    def _(j):
+        fill(leaf_msg, j, (me + j + 120) % 128)
+        near_send(j).start()
+
+    for i in range(5):
+        fill(leaf_msg, 17 + i, (me + JUMPS[i]) % 128)
+        jump_send(i).start()
+    fill(leaf_in, 8, me)
+
+    w_lo[...] = nn(n_lo[...], tlo[...])
+
+    wait_for(one_in, 7, one_r)
+
+    one_f[...] = one_in[...].astype(F32).reshape(64, 128)
+    for m in range(4):
+        two_msg[m] = jnp.concatenate(
+            [one_f[pl.ds(m * 2 + p, 8, stride=8), :] for p in range(2)], 0
+        ).astype(BF16)
+
+    def two_send(i):
+        peer = (yx + i) % 16
+        return send(two_msg, two_in.at[yx], two_s, two_r, peer * 8 + zc)
+
+    @pl.loop(1, 16)
+    def _(i):
+        two_send(i).start()
+
+    two_in[yx] = two_msg[...]
+
+    w_hi[...] = nn(n_hi[...], thi[...])
+
+    wait_for(window, 2, win_r)
     win_f[...] = window[...].astype(F32).reshape(96, 128)
     x_re = win_f[pl.ds(0, 48, stride=2), :]
     x_im = win_f[pl.ds(1, 48, stride=2), :]
@@ -319,19 +299,8 @@
     picked[...] = nn(select, values).astype(BF16)
 
     tile_copy.wait()
-    def leaf_sum(g):
-        base = g * 96
-        reals, imags = [], []
-        for b in range(4):
-            wr = w_lo[base : base + 88, b * 128 : (b + 1) * 128]
-            wi = w_lo[base : base + 88, 512 + b * 128 : 512 + (b + 1) * 128]
-            pr = p_lo[pl.ds(b, 88, stride=8), :]
-            pi = p_lo[pl.ds(4 + b, 88, stride=8), :]
-            reals.append(jnp.sum(wr * pr - wi * pi, 0, keepdims=True))
-            imags.append(jnp.sum(wr * pi + wi * pr, 0, keepdims=True))
-        inc_lo[g * 8 : g * 8 + 8, :] = jnp.concatenate(reals + imags, 0)
-
-    for grp in range(groups):
+
+    def near_group(grp):
         base = grp * GROUP
         x = picked[base : base + GROUP, :]
         lhs = jnp.concatenate([x[:, :256], x[:, 256:]], 0)
@@ -346,9 +315,56 @@
             for u in range(2):
                 total = total + jnp.where(local == 2 * q + u, res[:, u * 128 : (u + 1) * 128], 0.0)
         contrib[base : base + GROUP, :] = jnp.concatenate([total[:GROUP], total[GROUP:]], 1)
-        leaf_sum(grp)
-
-    for g in range(groups, 16):
+
+    for grp in range(12):
+        near_group(grp)
+
+    wait_for(two_in, 15, two_r)
+
+    for m in range(4):
+        for i in range(16):
+            hi_p[m, i * 16 : (i + 1) * 16, :] = two_in[i, m].astype(F32)
+
+    for c in range(8):
+        for p in range(2):
+            base = (c * 2 + p) * 256
+            for h in range(2):
+                wr = w_hi[base : base + 256, h * 128 : (h + 1) * 128]
+                wi = w_hi[base : base + 256, 256 + h * 128 : 256 + (h + 1) * 128]
+                pr = hi_p[h]
+                pi = hi_p[2 + h]
+                ret_msg[c, pl.ds(h * 2 + p, 1), :] = jnp.sum(wr * pr - wi * pi, 0, keepdims=True)
+                ret_msg[c, pl.ds(4 + h * 2 + p, 1), :] = jnp.sum(wr * pi + wi * pr, 0, keepdims=True)
+
+    def ret_send(i):
+        peer = (zc + i) % 8
+        return send(ret_msg.at[peer], ret_in.at[zc], ret_s, ret_r, yx * 8 + peer)
+
+    @pl.loop(1, 8)
+    def _(i):
+        ret_send(i).start()
+
+    ret_in[zc] = ret_msg[zc]
+
+    wait_for(leaf_in, 21, leaf_r)
+    p_lo[...] = leaf_in[...].astype(F32).reshape(704, 128)
+
+    def leaf_sum(g):
+        base = g * 96
+        reals, imags = [], []
+        for b in range(4):
+            wr = w_lo[base : base + 88, b * 128 : (b + 1) * 128]
+            wi = w_lo[base : base + 88, 512 + b * 128 : 512 + (b + 1) * 128]
+            pr = p_lo[pl.ds(b, 88, stride=8), :]
+            pi = p_lo[pl.ds(4 + b, 88, stride=8), :]
+            reals.append(jnp.sum(wr * pr - wi * pi, 0, keepdims=True))
+            imags.append(jnp.sum(wr * pi + wi * pr, 0, keepdims=True))
+        inc_lo[g * 8 : g * 8 + 8, :] = jnp.concatenate(reals + imags, 0)
+
+    for grp in range(12, groups):
+        near_group(grp)
+
+    for g in range(16):
         leaf_sum(g)
 
     whole = contrib[...]

time: 31.8 us -> 30.3 us (0.953)
  Pallas kernels: 30.8 us -> 29.5 us
    pallas_call x1, Pallas kernels: 30.8 us -> 29.5 us  [on_device(): pl.pallas_call(kernel, name='mlfmm', out_shape=pltpu.VMEM((32, 128), F32)...]
where the time goes in v4:
time: 30.3 us; the launch traced here: 30.1 us
  Pallas kernels  29.5 us (97%)
  other arithmetic  0.61 us (2%)
    pallas_call x1, Pallas kernels, on_device(): pl.pallas_call(kernel, name='mlfmm', out_shape=pltpu.VMEM((32, 128), F32)...  29.5 us
    add x1, other arithmetic, on_device(): res + 0.5 * density.reshape(32, 128).astype(F32)  0.61 us

profile of v4, /device:TPU:1, one launch (start us, length us, event | category | flops | bytes accessed | tf_op | source)
XLA Modules:
  0.0 30.1 jit_solution(16426416612969404792)
XLA Ops:
  0.0 0.0 copy-start
  0.0 29.5 %mlfmm.1 = f32[32,128]{1,0:T(8,128)S(1)} custom-call(bf16[32,128]{1,0:T(8,128)(2,1)} %bitcast.27, s32[4,128]{1,0:T(4,128)} %bitcast.29, s32[16,27]{1,0:T(8,128)} %near_src_h.1, s32[16,27]{1,0:T(8,128)} %near_tile_h.1, s32[16,189]{1,0:T(8,128)} %dps_h.1, s32[16,189]{1,0:T(8,128)} %ftype_h.1, s32[64,189]{1,0:T(8,128)} %pfar_h.1, s32[64,189]{1,0:T(8,128)} %ptype_h.1, ...), custom_call_target="tpu_custom_call" | custom-call | tf_op jit(solution)/shard_map/mlfmm/pallas_call | solution.py:428
  29.5 0.0 copy-done
  29.5 0.6 %multiply_add_fusion = f32[32,128]{1,0:T(8,128)} fusion(f32[32,128]{1,0:T(8,128)S(1)} %mlfmm.1, bf16[32,128]{1,0:T(8,128)(2,1)S(1)} %bitcast.28), kind=kLoop, calls=%fused_computation | loop fusion | flops 12288 | bytes 40960 | tf_op jit(solution)/shard_map/add | solution.py:510
Async XLA Ops:
  0.0 29.5 %copy-start = (bf16[16,2,128]{2,1,0:T(2,128)(2,1)S(1)}, bf16[16,2,128]{2,1,0:T(2,128)(2,1)}, u32[]{:S(2)}) copy-start(bf16[16,2,128]{2,1,0:T(2,128)(2,1)} %param.15) | copy-start | bytes 24580

commit v5 on v4

--- a/solution.py
+++ b/solution.py
@@ -11,7 +11,7 @@
 BF16 = jnp.bfloat16
 I32 = jnp.int32
 JUMPS = (16, 32, 64, 96, 112)
-TPAD = 384
+TPAD = 320
 GROUP = 16
 
 
@@ -40,10 +40,10 @@
 
 
 def kernel(
-    dens_h, sb, near_src_h, near_tile_h, dps_h, ftype_h, pfar_h, ptype_h, shift_h,
+    dens_h, sb_h, near_src_h, near_tile_h, dps_h, ftype_h, pfar_h, ptype_h, shift_h,
     radiate, receive, tiles, interp, lo_rows, hi_rows,
     out,
-    dens, near_src, near_tile, dps_in, ftype_in, pfar_in, ptype_in, shift_rows, small_sem,
+    sb, sb_sem, dens, near_src, near_tile, dps_in, ftype_in, pfar_in, ptype_in, shift_rows, small_sem,
     dens_f, win_f, nidx, dps, ftype, pfar, ptype, shifts, lo_v, hi_v, hi_f, tlo, thi, pat3, lo_sem, hi_sem,
     rad_v, rec_v, tile_v, int_v, window, patf, leaf_msg, leaf_in, hi_scr, one_msg, one_in, one_f,
     two_msg, two_in, hi_p, ret_msg, ret_in, down, n_lo, w_lo, p_lo, n_hi, w_hi, inc_lo, contrib, picked,
@@ -80,6 +80,8 @@
         c.start()
     rad_copy.start()
     int_copy.start()
+    box_copy = pltpu.make_async_copy(sb_h, sb, sb_sem)
+    box_copy.start()
     for c in small[3:]:
         c.start()
     lo_copy.start()
@@ -140,6 +142,7 @@
     for m in range(2):
         for b in range(4):
             patf[pl.ds(m * 4 + b, 16, stride=8), :] = pat_f[m * 16 : (m + 1) * 16, b * 128 : (b + 1) * 128]
+    box_copy.wait()
     pat3[...] = patf[...].reshape(16, 8, 128)
     small[3].wait()
     for m in range(2):
@@ -203,14 +206,14 @@
     def _(i):
         hi_f[pl.ds(pl.multiple_of(i * 1264, 16), 1264), :] = hi_v[pl.ds(i * 79, 79)].astype(F32).reshape(1264, 128)
 
-    hi_f[5056:, :] = jnp.zeros((1088, 128), F32)
+    hi_f[5056:, :] = jnp.zeros((64, 128), F32)
     for r in range(4):
         at = (r % 2) * 256 + (r // 2) * 128
         thi[:, at : at + 128] = hi_f[pl.ds((zc % 4) * 4 + r, TPAD, stride=16), :].astype(BF16)
 
     lo_copy.wait()
     hi_f[:2528, :] = lo_v[...].astype(F32)
-    hi_f[2528:3072, :] = jnp.zeros((544, 128), F32)
+    hi_f[2528:2560, :] = jnp.zeros((32, 128), F32)
     for r in range(8):
         at = (r % 2) * 512 + (r // 2) * 128
         tlo[:, at : at + 128] = hi_f[pl.ds(r, TPAD, stride=8), :].astype(BF16)
@@ -254,21 +257,6 @@
     low_copy.start()
     window[1] = dens[...]
 
-    @pl.loop(0, 8)
-    def _(j):
-        fill(leaf_msg, j, (me + j + 120) % 128)
-        near_send(j).start()
-
-    @pl.loop(9, 17)
-    def _(j):
-        fill(leaf_msg, j, (me + j + 120) % 128)
-        near_send(j).start()
-
-    for i in range(5):
-        fill(leaf_msg, 17 + i, (me + JUMPS[i]) % 128)
-        jump_send(i).start()
-    fill(leaf_in, 8, me)
-
     w_lo[...] = nn(n_lo[...], tlo[...])
 
     wait_for(one_in, 7, one_r)
@@ -288,6 +276,21 @@
         two_send(i).start()
 
     two_in[yx] = two_msg[...]
+
+    @pl.loop(0, 8)
+    def _(j):
+        fill(leaf_msg, j, (me + j + 120) % 128)
+        near_send(j).start()
+
+    @pl.loop(9, 17)
+    def _(j):
+        fill(leaf_msg, j, (me + j + 120) % 128)
+        near_send(j).start()
+
+    for i in range(5):
+        fill(leaf_msg, 17 + i, (me + JUMPS[i]) % 128)
+        jump_send(i).start()
+    fill(leaf_in, 8, me)
 
     w_hi[...] = nn(n_hi[...], thi[...])
 
@@ -429,9 +432,11 @@
         kernel,
         name="mlfmm",
         out_shape=pltpu.VMEM((32, 128), F32),
-        in_specs=[anyspace, pl.BlockSpec(memory_space=pltpu.SMEM)] + [anyspace] * 13,
+        in_specs=[anyspace] * 15,
         out_specs=vm,
         scratch_shapes=[
+            pltpu.SMEM((4, 128), I32),
+            dma,
             pltpu.VMEM((32, 128), BF16),
             pltpu.VMEM((16, 27), I32),
             pltpu.VMEM((16, 27), I32),

time: 30.3 us -> 29.8 us (0.983)
  Pallas kernels: 29.5 us -> 29.1 us
    pallas_call x1, Pallas kernels: 29.5 us -> 29.1 us  [on_device(): pl.pallas_call(kernel, name='mlfmm', out_shape=pltpu.VMEM((32, 128), F32)...]
where the time goes in v5:
time: 29.8 us; the launch traced here: 29.7 us
  Pallas kernels  29.1 us (98%)
  other arithmetic  0.61 us (2%)
    pallas_call x1, Pallas kernels, on_device(): pl.pallas_call(kernel, name='mlfmm', out_shape=pltpu.VMEM((32, 128), F32)...  29.1 us
    add x1, other arithmetic, on_device(): res + 0.5 * density.reshape(32, 128).astype(F32)  0.61 us

profile of v5, /device:TPU:1, one launch (start us, length us, event | category | flops | bytes accessed | tf_op | source)
XLA Modules:
  0.0 29.7 jit_solution(859970337585551816)
XLA Ops:
  0.0 0.0 copy-start
  0.0 29.1 %mlfmm.1 = f32[32,128]{1,0:T(8,128)S(1)} custom-call(bf16[32,128]{1,0:T(8,128)(2,1)} %bitcast.27, s32[4,128]{1,0:T(4,128)} %bitcast.29, s32[16,27]{1,0:T(8,128)} %near_src_h.1, s32[16,27]{1,0:T(8,128)} %near_tile_h.1, s32[16,189]{1,0:T(8,128)} %dps_h.1, s32[16,189]{1,0:T(8,128)} %ftype_h.1, s32[64,189]{1,0:T(8,128)} %pfar_h.1, s32[64,189]{1,0:T(8,128)} %ptype_h.1, ...), custom_call_target="tpu_custom_call" | custom-call | tf_op jit(solution)/shard_map/mlfmm/pallas_call | solution.py:431
  29.1 0.0 copy-done
  29.1 0.6 %multiply_add_fusion = f32[32,128]{1,0:T(8,128)} fusion(f32[32,128]{1,0:T(8,128)S(1)} %mlfmm.1, bf16[32,128]{1,0:T(8,128)(2,1)S(1)} %bitcast.28), kind=kLoop, calls=%fused_computation | loop fusion | flops 12288 | bytes 40960 | tf_op jit(solution)/shard_map/add | solution.py:515
Async XLA Ops:
  0.0 29.1 %copy-start = (bf16[16,2,128]{2,1,0:T(2,128)(2,1)S(1)}, bf16[16,2,128]{2,1,0:T(2,128)(2,1)}, u32[]{:S(2)}) copy-start(bf16[16,2,128]{2,1,0:T(2,128)(2,1)} %param.15) | copy-start | bytes 24580
